TPU v7x, 32 devices: a whole 2x2x4 slice. The times are simulated.
32 devices in a mesh: gx: 8 (over z, y), gy: 4 (over x, core).
Axes of the slice: x: 2, y: 2, z: 4, core: 2. Of those that a mesh axis runs over, the one named last changes fastest.
Arguments:
- inputs: bfloat16 [16, 16, 48, 128], P('gx', 'gy'), may hold values from -6 to 6
- cotangent: bfloat16 [16, 16, 48, 128], P('gx', 'gy'), may hold values from -6 to 6
- kernel: bfloat16 [27, 128, 128], replicated, may hold values from -0.109375 to 0.109375
Outputs:
- input_grad: bfloat16 [16, 16, 48, 128], P('gx', 'gy')
- kernel_grad: float32 [27, 128, 128], P(None, 'gx', 'gy')
All inputs are finite; a program needn't handle non-finite values.
Results may differ from a plain program's by a relative error of at most 0.0023.
Values may be sent and summed in bfloat16 or wider, within the bound.
No kernel may reach another device: no remote copies, remote signals or barrier semaphores. Data moves between devices by JAX's collectives and lax.ppermute only.
A program may use at most 64 MiB of HBM per device.

v0:
```python
import functools
import math

import jax
import jax.numpy as jnp
from jax import lax
from jax.experimental import pallas as pl
from jax.experimental.pallas import tpu as pltpu
from jax.sharding import PartitionSpec as P


AXES = ("gx", "gy")
BF16 = jnp.bfloat16
F32 = jnp.float32


def near_flips(chips):
    return [(1 << k) - 1 for k in range(1, chips.bit_length())]


def spot():
    at_x, at_y = lax.axis_index("gx"), lax.axis_index("gy")
    return at_x // 2, at_x % 2, at_y // 2, at_y % 2


def move(array, pairs):
    return lax.ppermute(array, AXES, pairs)


def swap(array, size, mask):
    return move(array, [(i, i ^ mask) for i in range(size)])


def pairs_along(count, stride, size, odd):
    found = []
    for i in range(size):
        at = (i // stride) % count
        to = at ^ 1 if not odd else (at - 1 if at % 2 == 0 else at + 1)
        if 0 <= to < count:
            found.append((i, i + (to - at) * stride))
    return found


def call(body, outs, args, scratch=(), flops=0, moved=0, fetch=False):
    vmem = pl.BlockSpec(memory_space=pltpu.VMEM)
    run = pl.pallas_call(
        body,
        out_shape=tuple(pltpu.VMEM(s, d) for s, d in outs),
        in_specs=[pl.BlockSpec(memory_space=pltpu.HBM) if fetch else vmem] * len(args),
        out_specs=tuple(vmem for _ in outs),
        scratch_shapes=list(scratch),
        compiler_params=pltpu.CompilerParams(vmem_limit_bytes=32 << 20),
        cost_estimate=pl.CostEstimate(flops=flops, bytes_accessed=moved, transcendentals=0),
    )
    space = pltpu.HBM if fetch else pltpu.VMEM
    args = [pltpu.with_memory_space_constraint(a, space) for a in args]
    return run(*args)


def gelu_parts(values):
    cdf = 0.5 * (1.0 + lax.erf(values / math.sqrt(2.0)))
    return cdf


def pack_body(dims, inputs_hbm, cot_hbm, *refs):
    parts_x, parts_y, wx, wy, depth, chans = dims
    _, lo, chip, core = spot()
    chips = parts_y // 2
    block_i, half = chans // parts_x, chans // 2
    block_o = chans // parts_y
    rows = wx * wy * depth
    *outs, inputs_ref, cot_ref, arrived = refs
    copies = [
        pltpu.make_async_copy(inputs_hbm, inputs_ref, arrived.at[0]),
        pltpu.make_async_copy(cot_hbm, cot_ref, arrived.at[1]),
    ]
    for copy in copies:
        copy.start()
    for copy in copies:
        copy.wait()
    outs[-2][...] = cot_ref[lo * (wx - 1)].reshape(wy * depth, chans)
    outs[-1][...] = cot_ref[(1 - lo) * (wx - 1)].reshape(wy * depth, chans)
    for flip in [0, *near_flips(chips)]:
        column = (core if flip else 1 - core) * (wy - 1)
        for x in range(wx):
            plane = cot_ref[x, column]
            outs[flip][rows + x * depth : rows + (x + 1) * depth] = plane
            outs[chips + flip][rows + x * depth : rows + (x + 1) * depth] = plane
    values = inputs_ref[...].reshape(rows, chans).astype(F32)
    act = (values * gelu_parts(values)).astype(BF16)
    both = jnp.concatenate([act, cot_ref[...].reshape(rows, chans)], axis=1)
    lane = lax.broadcasted_iota(jnp.int32, (1, chans), 1)
    at = lax.broadcasted_iota(jnp.int32, (2 * chans, chans), 0)
    group = jnp.right_shift(lane, block_i.bit_length() - 1)
    column = lane - half
    side = jnp.right_shift(column, block_o.bit_length() - 1) ^ core
    for flip_lo in range(2):
        for flip in range(chips):
            to_lo, to_chip = lo ^ flip_lo, chip ^ flip
            from_act = (2 * group + to_lo) * block_i + (lane & (block_i - 1))
            from_cot = (2 * to_chip + side) * block_o + (column & (block_o - 1))
            from_cot = jnp.where(column < 2 * block_o, chans + from_cot, -1)
            chosen = (at == jnp.where(lane < half, from_act, from_cot)).astype(F32).astype(BF16)
            out = outs[flip_lo * chips + flip]
            out[:rows] = jnp.dot(both, chosen, preferred_element_type=F32).astype(BF16)


def in_lanes(value, shift, slot, width, lane):
    chans = value.shape[1]
    moved = pltpu.roll(value, shift % chans, 1) if shift % chans else value
    keep = (lane >= slot * width) & (lane < (slot + 1) * width)
    return jnp.where(keep, moved, 0.0).astype(BF16)


def unpack_body(dims, *refs):
    _, parts_y, wx, wy, depth, chans = dims
    hi, lo, chip, core = spot()
    chips, half, block_o = parts_y // 2, chans // 2, chans // parts_y
    blocks, cot_ref = refs[: 4 * chips], refs[4 * chips]
    acts, wide, even, odd, pad, cots = refs[4 * chips + 1 :]
    rows = wx * wy * depth
    total_y, strip = wy * parts_y, wy * depth
    lane = lax.broadcasted_iota(jnp.int32, (1, chans), 1)
    blank = jnp.zeros((depth, chans), BF16)
    for x in range(2 * wx):
        for slot in range(3):
            cots[slot, x, 0] = blank
            cots[slot, x, total_y + 1] = blank
    facing = (1 - lo) * (wx + 1)
    toward, away = (1 - core) * (wy + 1), core * (wy + 1)
    swapped = blocks[2 * chips :]
    pad[1 : wx + 1, 1 : wy + 1] = cot_ref[...]
    near_row = pl.multiple_of(rows + lo * (wx - 1) * depth, depth)
    far_row = pl.multiple_of(rows + (1 - lo) * (wx - 1) * depth, depth)
    size = total_y // 4 * depth
    pad[facing, toward] = swapped[chips][pl.ds(near_row, depth)]
    pad[facing, away] = blank
    for out in (even, odd):
        out[size : size + depth] = swapped[chips][pl.ds(far_row, depth)]
        out[size + depth :] = blank
    for x in range(wx):
        pad[x + 1, toward] = swapped[0][rows + x * depth : rows + (x + 1) * depth]
        pad[x + 1, away] = blank
    for flip in near_flips(chips):

        @pl.when((chip ^ flip) == chip + 2 * core - 1)
        def _(flip=flip):
            pad[facing, away] = swapped[chips + flip][pl.ds(near_row, depth)]
            for out in (even, odd):
                out[size + depth :] = swapped[chips + flip][pl.ds(far_row, depth)]
            for x in range(wx):
                pad[x + 1, away] = swapped[flip][rows + x * depth : rows + (x + 1) * depth]

    place = 0
    for flip_core in range(2):
        for flip_lo in range(2):
            for flip in range(chips):
                block = blocks[place]
                place += 1
                first_x = (lo ^ flip_lo) * wx
                first_y = (2 * (chip ^ flip) + (core ^ flip_core)) * wy
                for x in range(wx):
                    part = block[x * strip : (x + 1) * strip]
                    acts[first_x + x, pl.ds(first_y, wy)] = part.reshape(wy, depth, chans)
                    value = part.astype(F32)
                    for slot in range(3):
                        shift = (slot - flip_core) * block_o - half
                        cots[slot, first_x + x, pl.ds(first_y + 1, wy)] = in_lanes(
                            value, shift, slot, block_o, lane
                        ).reshape(wy, depth, chans)

    def merge(y, carry):
        for x in range(2 * wx):
            wide[x + 1, y] = cots[0, x, y + 2] + cots[1, x, y + 1] + cots[2, x, y]
        wide[0, y] = blank
        wide[2 * wx + 1, y] = blank
        return carry

    lax.fori_loop(0, total_y, merge, 0, unroll=4)
    part_y = total_y // 4
    for out, x in ((even, (1 - hi % 2) * (2 * wx - 1)), (odd, (hi % 2) * (2 * wx - 1))):
        total = cots[0, x, 1 : 1 + part_y] + cots[1, x, 1 + part_y : 1 + 2 * part_y]
        total = total + cots[2, x, 1 + 2 * part_y : 1 + 3 * part_y]
        last = cots[0, x, 1 + 3 * part_y : 1 + 4 * part_y].reshape(size, chans).astype(F32)
        last = pltpu.roll(last, 3 * block_o, 1).astype(BF16)
        out[:size] = total.reshape(size, chans) + last


def main_body(dims, acts, wide, sums, low, high):
    _, parts_y, wx, wy, depth, chans = dims
    half, total_y = chans // 2, wy * parts_y
    step = min(total_y, 16)
    z = lax.broadcasted_iota(jnp.int32, (depth, 1), 0)
    sums[...] = jnp.zeros_like(sums)
    for x in range(2 * wx):

        def chunk(n, carry, x=x):
            planes = pl.ds(n * step, step)
            middle = acts[x, planes][:, :, :half].astype(F32)
            below = jnp.where(z > 0, pltpu.roll(middle, 1, 1), 0.0)
            above = jnp.where(z < depth - 1, pltpu.roll(middle, depth - 1, 1), 0.0)
            left = jnp.concatenate([below, middle, above], axis=2).astype(BF16)
            left = left.reshape(step * depth, 3 * half)
            if x == 0:
                low[pl.ds(pl.multiple_of(n * step * depth, step * depth), step * depth)] = left
            if x == 2 * wx - 1:
                high[pl.ds(pl.multiple_of(n * step * depth, step * depth), step * depth)] = left
            right = jnp.concatenate(
                [wide[x + 2 - jx, planes].reshape(step * depth, chans) for jx in range(3)], axis=1
            )
            sums[...] += lax.dot_general(
                left, right, (((0,), (0,)), ((), ())), preferred_element_type=F32
            )
            return carry

        if total_y == step:
            chunk(0, 0)
        else:
            lax.fori_loop(0, total_y // step, chunk, 0)


def ends_body(dims, main_ref, low, high, even, odd, *refs):
    parts_x, parts_y, _, wy, depth, chans = dims
    hi, _, _, _ = spot()
    his = parts_x // 2
    block_i, half, block_o = chans // parts_x, chans // 2, chans // parts_y
    outs, (cots, sums) = refs[:his], refs[his:]
    total_y = wy * parts_y
    part_y = total_y // 4
    size = part_y * depth
    lane = lax.broadcasted_iota(jnp.int32, (1, chans), 1)
    blank = jnp.zeros((depth, chans), BF16)
    for end in range(2):
        for slot in range(3):
            cots[end, slot, 0] = blank
            cots[end, slot, total_y + 1] = blank
    for ref, end in ((even, 1 - hi % 2), (odd, hi % 2)):
        value = ref[:size].astype(F32)
        for slot in range(3):
            for part in range(4):
                cots[end, slot, 1 + part * part_y : 1 + (part + 1) * part_y] = in_lanes(
                    value, (slot - part) * block_o, slot, block_o, lane
                ).reshape(part_y, depth, chans)
    sums[...] = main_ref[...]
    for end, left, jx in ((0, low, 2), (1, high, 0)):
        right = cots[end, 0, 2 : total_y + 2] + cots[end, 1, 1 : total_y + 1]
        right = right + cots[end, 2, 0:total_y]
        sums[:, jx * chans : (jx + 1) * chans] += lax.dot_general(
            left[...],
            right.reshape(total_y * depth, chans),
            (((0,), (0,)), ((), ())),
            preferred_element_type=F32,
        )
    free = 3 * block_o
    for flip, out in enumerate(outs):
        start = pl.multiple_of((hi ^ flip) * block_i, block_i)

        def group(jx, jz):
            return sums[pl.ds(jz * half + start, block_i), jx * chans : (jx + 1) * chans]

        last = jnp.zeros((block_i, chans), F32)
        for jz in range(3):
            spare = group(2, jz)
            for jx in range(2):
                moved = pltpu.roll(spare, free - jx * block_o, 1)
                piece = jnp.where(lane < free, group(jx, jz), moved)
                out[(3 * jx + jz) * block_i : (3 * jx + jz + 1) * block_i] = piece.astype(out.dtype)
            moved = pltpu.roll(spare, ((jz - 2) * block_o) % chans, 1)
            keep = (lane >= jz * block_o) & (lane < (jz + 1) * block_o)
            last = jnp.where(keep, moved, last)
        out[6 * block_i :] = last.astype(out.dtype)


def back_body(dims, inputs_ref, pad_ref, outer_ref, inner_ref, even, odd, kernel_ref, out_ref, pad):
    _, parts_y, wx, wy, depth, chans = dims
    hi, lo, _, core = spot()
    rows = wx * wy * depth
    pad[...] = pad_ref[...]
    pad[(1 - lo) * (wx + 1), 1 : wy + 1] = inner_ref[...].reshape(wy, depth, chans)
    pad[lo * (wx + 1), 1 : wy + 1] = outer_ref[...].reshape(wy, depth, chans)
    toward, away = (1 - core) * (wy + 1), core * (wy + 1)
    size = wy * parts_y // 4 * depth
    for ref, parity in ((even, 1), (odd, 0)):

        @pl.when((hi + lo) % 2 == parity)
        def _(ref=ref):
            pad[lo * (wx + 1), toward] = ref[size : size + depth]
            pad[lo * (wx + 1), away] = ref[size + depth :]

    left, right = [], []
    for jx in range(3):
        for jy in range(3):
            first = jx * 9 + jy * 3
            piece = pad[2 - jx : 2 - jx + wx, 2 - jy : 2 - jy + wy]
            left.append(piece.reshape(rows, chans))
            right.append(kernel_ref[first : first + 3].reshape(3 * chans, chans))
    product = lax.dot_general(
        jnp.concatenate(left, axis=1),
        jnp.concatenate(right, axis=1),
        (((1,), (1,)), ((), ())),
        preferred_element_type=F32,
    ).reshape(wx * wy, depth, 3 * chans)
    z = lax.broadcasted_iota(jnp.int32, (depth, 1), 0)
    low = product[:, :, :chans]
    high = product[:, :, 2 * chans :]
    back = product[:, :, chans : 2 * chans]
    back += jnp.where(z < depth - 1, pltpu.roll(low, depth - 1, 1), 0.0)
    back += jnp.where(z > 0, pltpu.roll(high, 1, 1), 0.0)
    values = inputs_ref[...].astype(F32).reshape(wx * wy, depth, chans)
    cdf = gelu_parts(values)
    slope = cdf + values * jnp.exp(-0.5 * values * values) / math.sqrt(2.0 * math.pi)
    out_ref[...] = (slope * back).astype(BF16).reshape(wx, wy, depth, chans)


def final_body(dims, voxels, *refs):
    parts_x, parts_y, _, _, _, chans = dims
    block_i, block_o = chans // parts_x, chans // parts_y
    out = refs[-1]
    total = refs[0][...]
    for ref in refs[1:-1]:
        total = total + ref[...].astype(F32)
    total = total * (1.0 / math.sqrt(voxels))
    for jx in range(3):
        for jy in range(3):
            for jz in range(3):
                if jx < 2:
                    row, column = 3 * jx + jz, jy
                elif jy < 2:
                    row, column = 3 * jy + jz, 3
                else:
                    row, column = 6, jz
                out[9 * jx + 3 * jy + jz] = total[
                    row * block_i : (row + 1) * block_i, column * block_o : (column + 1) * block_o
                ]


def local(inputs, cotangent, kernel):
    wx, wy, depth, chans = inputs.shape
    parts_x, parts_y = lax.axis_size("gx"), lax.axis_size("gy")
    size = parts_x * parts_y
    his, chips = parts_x // 2, parts_y // 2
    dims = (parts_x, parts_y, wx, wy, depth, chans)
    rows = wx * wy * depth
    block_i, half = chans // parts_x, chans // 2
    total_y, total_x = wy * parts_y, 2 * wx
    face = (wy * depth, chans)
    near = [0, *near_flips(chips)]
    extras = [rows + wx * depth * (n % chips in near) for n in range(2 * chips)]

    count = 2 * chips
    *packed, outer, inner = call(
        functools.partial(pack_body, dims),
        [((n, chans), BF16) for n in extras] + [(face, BF16)] * 2,
        (inputs, cotangent),
        scratch=(
            pltpu.VMEM(inputs.shape, BF16),
            pltpu.VMEM(inputs.shape, BF16),
            pltpu.SemaphoreType.DMA((2,)),
        ),
        fetch=True,
        flops=2 * count * rows * 2 * chans * chans,
        moved=2 * (count + 3) * rows * chans,
    )
    masks = [a * parts_y + 2 * g for a in range(2) for g in range(chips)]
    same = [packed[0]] + [swap(packed[n], size, masks[n]) for n in range(1, count)]
    other = [swap(same[n], size, 1) for n in range(count)]
    outer = move(outer, pairs_along(parts_x, parts_y, size, True))
    inner = move(inner, pairs_along(parts_x, parts_y, size, False))

    acts, wide, end_even, end_odd, pad = call(
        functools.partial(unpack_body, dims),
        [
            ((total_x, total_y, depth, chans), BF16),
            ((total_x + 2, total_y, depth, chans), BF16),
            (((total_y // 4 + 2) * depth, chans), BF16),
            (((total_y // 4 + 2) * depth, chans), BF16),
            ((wx + 2, wy + 2, depth, chans), BF16),
        ],
        (*same, *other, cotangent),
        scratch=(pltpu.VMEM((3, total_x, total_y + 2, depth, chans), BF16),),
        moved=4 * count * rows * chans,
    )
    end_even = move(end_even, pairs_along(his, 2 * parts_y, size, False))
    end_odd = move(end_odd, pairs_along(his, 2 * parts_y, size, True))
    sums, low, high = call(
        functools.partial(main_body, dims),
        [((3 * half, 3 * chans), F32), ((total_y * depth, 3 * half), BF16), ((total_y * depth, 3 * half), BF16)],
        (acts, wide),
        flops=2 * total_x * total_y * depth * 9 * half * chans,
        moved=4 * count * rows * chans,
    )
    raw = call(
        functools.partial(ends_body, dims),
        [((7 * block_i, chans), BF16 if m else F32) for m in range(his)],
        (sums, low, high, end_even, end_odd),
        scratch=(
            pltpu.VMEM((2, 3, total_y + 2, depth, chans), BF16),
            pltpu.VMEM((3 * half, 3 * chans), F32),
        ),
        flops=4 * total_y * depth * 3 * half * chans,
        moved=4 * total_y * depth * chans,
    )
    terms = [raw[0]] + [swap(raw[m], size, m * 2 * parts_y) for m in range(1, his)]
    (input_grad,) = call(
        functools.partial(back_body, dims),
        [((wx, wy, depth, chans), BF16)],
        (inputs, pad, outer, inner, end_even, end_odd, kernel),
        scratch=(pltpu.VMEM((wx + 2, wy + 2, depth, chans), BF16),),
        flops=2 * rows * 27 * chans * chans,
        moved=2 * 27 * chans * chans,
    )
    voxels = wx * parts_x * wy * parts_y * depth
    (kernel_grad,) = call(
        functools.partial(final_body, dims, voxels),
        [((27, block_i, chans // parts_y), F32)],
        terms,
        moved=4 * his * 7 * block_i * chans,
    )
    return (input_grad, kernel_grad)


def solution(mesh):
    return jax.shard_map(
        local,
        mesh=mesh,
        in_specs=(P("gx", "gy", None, None), P("gx", "gy", None, None), P()),
        out_specs=(P("gx", "gy", None, None), P(None, "gx", "gy")),
        check_vma=False,
    )
```

profile of v0, /device:TPU:0, one launch (start us, length us, event | category | flops | bytes accessed | tf_op | source)
XLA Modules:
  0.0 35.9 jit_solution(261585692578542152)
XLA Ops:
  0.6 1.4 %shard_map.50 = (bf16[480,128]{1,0:T(8,128)(2,1)S(1)}, bf16[480,128]{1,0:T(8,128)(2,1)S(1)}, bf16[480,128]{1,0:T(8,128)(2,1)S(1)}, bf16[480,128]{1,0:T(8,128)(2,...) custom-call(bf16[2,4,48,128]{3,2,1,0:T(8,128)(2,1)} %inputs_ref.1, bf16[2,4,48,128]{3,2,1,0:T(8,128)(2,1)} %refs_8_.1), custom_call_target="tpu_custom_call" | custom-call | flops 100663296 | bytes 688128 | tf_op jit(solution)/shard_map/pallas_call | solution.py:57
  2.0 3.0 %collective-permute-start = (bf16[480,128]{1,0:T(8,128)(2,1)S(1)}, bf16[480,128]{1,0:T(8,128)(2,1)S(1)}, u32[]{:S(2)}, u32[]{:S(2)}) collective-permute-start(bf16[480,128]{1,0:T(8,128)(2,1)S(1)} %get-tuple-element.21), channel_id=1, source_target_pairs={{0,2},{1,3},{2,0},{3,1},{4,6},{5,7},{6,4},{7,5},{8,10},{9,11},{10,... | collective-permute-start | bytes 368648 | tf_op jit(solution)/shard_map/ppermute | solution.py:27
  5.0 1.5 %collective-permute-start.1 = (bf16[480,128]{1,0:T(8,128)(2,1)S(1)}, bf16[480,128]{1,0:T(8,128)(2,1)S(1)}, u32[]{:S(2)}, u32[]{:S(2)}) collective-permute-start(bf16[480,128]{1,0:T(8,128)(2,1)S(1)} %get-tuple-element.22), channel_id=1, source_target_pairs={{0,4},{1,5},{2,6},{3,7},{4,0},{5,1},{6,2},{7,3},{8,12},{9,13},{10,... | collective-permute-start | bytes 368648 | tf_op jit(solution)/shard_map/ppermute | solution.py:27
  6.5 0.0 collective-permute-start.2
  6.6 0.0 collective-permute-start.3
  6.6 2.2 %collective-permute-done.refs_1_ = bf16[480,128]{1,0:T(8,128)(2,1)S(1)} collective-permute-done((bf16[480,128]{1,0:T(8,128)(2,1)S(1)}, bf16[480,128]{1,0:T(8,128)(2,1)S(1)}, u32[]{:S(2)}, u32[]{:S(2)}) %collective-permute-start) | collective-permute-done | bytes 122912 | tf_op jit(solution)/shard_map/ppermute | solution.py:27
  8.7 3.8 %collective-permute-done.1.refs_2_ = bf16[480,128]{1,0:T(8,128)(2,1)S(1)} collective-permute-done((bf16[480,128]{1,0:T(8,128)(2,1)S(1)}, bf16[480,128]{1,0:T(8,128)(2,1)S(1)}, u32[]{:S(2)}, u32[]{:S(2)}) %collective-permute-start.1) | collective-permute-done | bytes 122912 | tf_op jit(solution)/shard_map/ppermute | solution.py:27
  12.5 0.0 collective-permute-done.2.refs_3_
  12.5 0.5 %collective-permute-start.6 = (bf16[480,128]{1,0:T(8,128)(2,1)S(1)}, bf16[480,128]{1,0:T(8,128)(2,1)S(1)}, u32[]{:S(2)}, u32[]{:S(2)}) collective-permute-start(bf16[480,128]{1,0:T(8,128)(2,1)S(1)} %collective-permute-done.2.refs_3_), channel_id=1, source_target_pairs={{0,1},{1,0},{2,3},{3,2},{4,5},{5,4},{6,7},{7,6},{8,9},{9,8},{10,11... | collective-permute-start | bytes 368648 | tf_op jit(solution)/shard_map/ppermute | solution.py:27
  13.1 0.0 collective-permute-done.3.refs_4_
  13.1 0.0 collective-permute-done.4.refs_5_
  13.1 0.8 %collective-permute-done.5.refs_6_ = bf16[480,128]{1,0:T(8,128)(2,1)S(1)} collective-permute-done((bf16[480,128]{1,0:T(8,128)(2,1)S(1)}, bf16[480,128]{1,0:T(8,128)(2,1)S(1)}, u32[]{:S(2)}, u32[]{:S(2)}) %collective-permute-start.5) | collective-permute-done | bytes 122912 | tf_op jit(solution)/shard_map/ppermute | solution.py:27
  13.9 0.2 collective-permute-done.6.refs_7_
  14.1 0.9 %copy-done.1 = bf16[2,4,48,128]{3,2,1,0:T(8,128)(2,1)S(1)} copy-done((bf16[2,4,48,128]{3,2,1,0:T(8,128)(2,1)S(1)}, bf16[2,4,48,128]{3,2,1,0:T(8,128)(2,1)}, u32[]{:S(2)}) %copy-start.1) | copy-done | bytes 98328
  14.9 1.1 %shard_map.51 = (bf16[4,16,48,128]{3,2,1,0:T(8,128)(2,1)S(1)}, bf16[6,16,48,128]{3,2,1,0:T(8,128)(2,1)S(1)}, bf16[288,128]{1,0:T(8,128)(2,1)S(1)}, bf16[288,128]...) custom-call(bf16[480,128]{1,0:T(8,128)(2,1)S(1)} %get-tuple-element.20.refs_0_, ...), custom_call_target="tpu_custom_call" | custom-call | bytes 786432 | tf_op jit(solution)/shard_map/pallas_call | solution.py:57
  16.0 1.6 %collective-permute-start.9 = (bf16[288,128]{1,0:T(8,128)(2,1)S(1)}, bf16[288,128]{1,0:T(8,128)(2,1)S(1)}, u32[]{:S(2)}, u32[]{:S(2)}) collective-permute-start(bf16[288,128]{1,0:T(8,128)(2,1)S(1)} %get-tuple-element.27), channel_id=1, source_target_pairs={{0,8},{1,9},{2,10},{3,11},{4,12},{5,13},{6,14},{7,15},{8,0},{9,1},... | collective-permute-start | bytes 221192 | tf_op jit(solution)/shard_map/ppermute | solution.py:27
  17.6 0.7 %collective-permute-start.10 = (bf16[288,128]{1,0:T(8,128)(2,1)S(1)}, bf16[288,128]{1,0:T(8,128)(2,1)S(1)}, u32[]{:S(2)}, u32[]{:S(2)}) collective-permute-start(bf16[288,128]{1,0:T(8,128)(2,1)S(1)} %get-tuple-element.28), channel_id=1, source_target_pairs={{8,16},{9,17},{10,18},{11,19},{12,20},{13,21},{14,22},{15,23},{16,... | collective-permute-start | bytes 221192 | tf_op jit(solution)/shard_map/ppermute | solution.py:27
  18.3 0.7 %collective-permute-start.7 = (bf16[192,128]{1,0:T(8,128)(2,1)S(1)}, bf16[192,128]{1,0:T(8,128)(2,1)S(1)}, u32[]{:S(2)}, u32[]{:S(2)}) collective-permute-start(bf16[192,128]{1,0:T(8,128)(2,1)S(1)} %get-tuple-element.25), channel_id=1, source_target_pairs={{4,8},{5,9},{6,10},{7,11},{8,4},{9,5},{10,6},{11,7},{12,16},{13,17... | collective-permute-start | bytes 147464 | tf_op jit(solution)/shard_map/ppermute | solution.py:27
  19.0 7.2 %collective-permute-start.8 = (bf16[192,128]{1,0:T(8,128)(2,1)S(1)}, bf16[192,128]{1,0:T(8,128)(2,1)S(1)}, u32[]{:S(2)}, u32[]{:S(2)}) collective-permute-start(bf16[192,128]{1,0:T(8,128)(2,1)S(1)} %get-tuple-element.26), channel_id=1, source_target_pairs={{0,4},{1,5},{2,6},{3,7},{4,0},{5,1},{6,2},{7,3},{8,12},{9,13},{10,... | collective-permute-start | bytes 147464 | tf_op jit(solution)/shard_map/ppermute | solution.py:27
  26.2 1.4 %shard_map.53 = (f32[192,384]{1,0:T(8,128)S(1)}, bf16[768,192]{1,0:T(8,128)(2,1)S(1)}, bf16[768,192]{1,0:T(8,128)(2,1)S(1)}) custom-call(bf16[4,16,48,128]{3,2,1,0:T(8,128)(2,1)S(1)} %get-tuple-element.29.acts, bf16[6,16,48,128]{3,2,1,0:T(8,128)(2,1)S(1)} %get-tuple-element.30.wide), custom_call_target="tpu_custom_call" | custom-call | flops 452984832 | bytes 786432 | tf_op jit(solution)/shard_map/pallas_call | solution.py:57
  27.6 0.0 collective-permute-done.10.odd
  27.6 0.7 %shard_map.54 = (f32[112,128]{1,0:T(8,128)S(1)}, bf16[112,128]{1,0:T(8,128)(2,1)S(1)}, bf16[112,128]{1,0:T(8,128)(2,1)S(1)}, bf16[112,128]{1,0:T(8,128)(2,1)S(1)}) custom-call(f32[192,384]{1,0:T(8,128)S(1)} %get-tuple-element.31.main_ref, bf16[768,192]{1,0:T(8,128)(2,1)S(1)} %get-tuple-element.32.low, bf16[768,192]{1,0:T(8,128)(2,1)S(1)} %get-tuple-element.33.high, ...), custom_call_target="tpu_custom_call" | custom-call | flops 75497472 | bytes 393216 | tf_op jit(solution)/shard_map/pallas_call | solution.py:57
  28.3 0.1 collective-permute-start.11
  28.4 1.0 %collective-permute-start.12 = (bf16[112,128]{1,0:T(8,128)(2,1)S(1)}, bf16[112,128]{1,0:T(8,128)(2,1)S(1)}, u32[]{:S(2)}, u32[]{:S(2)}) collective-permute-start(bf16[112,128]{1,0:T(8,128)(2,1)S(1)} %get-tuple-element.36), channel_id=1, source_target_pairs={{0,16},{1,17},{2,18},{3,19},{4,20},{5,21},{6,22},{7,23},{8,24},{9,... | collective-permute-start | bytes 86024 | tf_op jit(solution)/shard_map/ppermute | solution.py:27
  29.4 3.4 %collective-permute-start.13 = (bf16[112,128]{1,0:T(8,128)(2,1)S(1)}, bf16[112,128]{1,0:T(8,128)(2,1)S(1)}, u32[]{:S(2)}, u32[]{:S(2)}) collective-permute-start(bf16[112,128]{1,0:T(8,128)(2,1)S(1)} %get-tuple-element.37), channel_id=1, source_target_pairs={{0,24},{1,25},{2,26},{3,27},{4,28},{5,29},{6,30},{7,31},{8,16},{9,... | collective-permute-start | bytes 86024 | tf_op jit(solution)/shard_map/ppermute | solution.py:27
  32.8 0.7 %shard_map.52 = bf16[2,4,48,128]{3,2,1,0:T(8,128)(2,1)S(1)} custom-call(bf16[2,4,48,128]{3,2,1,0:T(8,128)(2,1)S(1)} %copy-done.2, bf16[4,6,48,128]{3,2,1,0:T(8,128)(2,1)S(1)} %get-tuple-element.24.pad_ref, bf16[192,128]{1,0:T(8,128)(2,1)S(1)} %collective-permute-done.7.outer_ref, bf16[192,128]{1,0:T(8,128)(2,1)S(1)} %collective-permute-done.8.inner_ref, ...), custom_call_target="tpu_custom_call" | custom-call | flops 339738624 | bytes 884736 | tf_op jit(solution)/shard_map/pallas_call | solution.py:57
  33.5 0.6 %copy.5 = bf16[2,4,48,128]{3,2,1,0:T(8,128)(2,1)} copy(bf16[2,4,48,128]{3,2,1,0:T(8,128)(2,1)S(1)} %shard_map.52) | data formatting | bytes 196608
  34.2 0.0 collective-permute-done.11.refs_1_
  34.2 0.0 collective-permute-done.12.refs_2_
  34.2 0.9 %collective-permute-done.13.refs_3_ = bf16[112,128]{1,0:T(8,128)(2,1)S(1)} collective-permute-done((bf16[112,128]{1,0:T(8,128)(2,1)S(1)}, bf16[112,128]{1,0:T(8,128)(2,1)S(1)}, u32[]{:S(2)}, u32[]{:S(2)}) %collective-permute-start.13) | collective-permute-done | bytes 28704 | tf_op jit(solution)/shard_map/ppermute | solution.py:27
  35.1 0.1 shard_map.55
  35.2 0.7 %copy.6 = f32[27,16,32]{2,1,0:T(8,128)} copy(f32[27,16,32]{2,1,0:T(8,128)S(1)} %shard_map.55) | data formatting | bytes 110592
  (10 shorter events, 0.0 us)
Async XLA Ops:
  2.0 6.7 %collective-permute-start = (bf16[480,128]{1,0:T(8,128)(2,1)S(1)}, bf16[480,128]{1,0:T(8,128)(2,1)S(1)}, u32[]{:S(2)}, u32[]{:S(2)}) collective-permute-start(bf16[480,128]{1,0:T(8,128)(2,1)S(1)} %get-tuple-element.21), channel_id=1, source_target_pairs={{0,2},{1,3},{2,0},{3,1},{4,6},{5,7},{6,4},{7,5},{8,10},{9,11},{10,... | collective-permute-start | bytes 368648 | tf_op jit(solution)/shard_map/ppermute | solution.py:27
  5.0 7.5 %collective-permute-start.1 = (bf16[480,128]{1,0:T(8,128)(2,1)S(1)}, bf16[480,128]{1,0:T(8,128)(2,1)S(1)}, u32[]{:S(2)}, u32[]{:S(2)}) collective-permute-start(bf16[480,128]{1,0:T(8,128)(2,1)S(1)} %get-tuple-element.22), channel_id=1, source_target_pairs={{0,4},{1,5},{2,6},{3,7},{4,0},{5,1},{6,2},{7,3},{8,12},{9,13},{10,... | collective-permute-start | bytes 368648 | tf_op jit(solution)/shard_map/ppermute | solution.py:27
  6.5 6.0 %collective-permute-start.2 = (bf16[480,128]{1,0:T(8,128)(2,1)S(1)}, bf16[480,128]{1,0:T(8,128)(2,1)S(1)}, u32[]{:S(2)}, u32[]{:S(2)}) collective-permute-start(bf16[480,128]{1,0:T(8,128)(2,1)S(1)} %get-tuple-element.23), channel_id=1, source_target_pairs={{0,6},{1,7},{2,4},{3,5},{4,2},{5,3},{6,0},{7,1},{8,14},{9,15},{10,... | collective-permute-start | bytes 368648 | tf_op jit(solution)/shard_map/ppermute | solution.py:27
  6.6 6.5 %collective-permute-start.3 = (bf16[480,128]{1,0:T(8,128)(2,1)S(1)}, bf16[480,128]{1,0:T(8,128)(2,1)S(1)}, u32[]{:S(2)}, u32[]{:S(2)}) collective-permute-start(bf16[480,128]{1,0:T(8,128)(2,1)S(1)} %get-tuple-element.20.refs_0_), channel_id=1, source_target_pairs={{0,1},{1,0},{2,3},{3,2},{4,5},{5,4},{6,7},{7,6},{8,9},{9,8},{10,11... | collective-permute-start | bytes 368648 | tf_op jit(solution)/shard_map/ppermute | solution.py:27
  8.7 4.3 %collective-permute-start.4 = (bf16[480,128]{1,0:T(8,128)(2,1)S(1)}, bf16[480,128]{1,0:T(8,128)(2,1)S(1)}, u32[]{:S(2)}, u32[]{:S(2)}) collective-permute-start(bf16[480,128]{1,0:T(8,128)(2,1)S(1)} %collective-permute-done.refs_1_), channel_id=1, source_target_pairs={{0,1},{1,0},{2,3},{3,2},{4,5},{5,4},{6,7},{7,6},{8,9},{9,8},{10,11... | collective-permute-start | bytes 368648 | tf_op jit(solution)/shard_map/ppermute | solution.py:27
  12.5 1.3 %collective-permute-start.5 = (bf16[480,128]{1,0:T(8,128)(2,1)S(1)}, bf16[480,128]{1,0:T(8,128)(2,1)S(1)}, u32[]{:S(2)}, u32[]{:S(2)}) collective-permute-start(bf16[480,128]{1,0:T(8,128)(2,1)S(1)} %collective-permute-done.1.refs_2_), channel_id=1, source_target_pairs={{0,1},{1,0},{2,3},{3,2},{4,5},{5,4},{6,7},{7,6},{8,9},{9,8},{10,11... | collective-permute-start | bytes 368648 | tf_op jit(solution)/shard_map/ppermute | solution.py:27
  12.5 1.5 %collective-permute-start.6 = (bf16[480,128]{1,0:T(8,128)(2,1)S(1)}, bf16[480,128]{1,0:T(8,128)(2,1)S(1)}, u32[]{:S(2)}, u32[]{:S(2)}) collective-permute-start(bf16[480,128]{1,0:T(8,128)(2,1)S(1)} %collective-permute-done.2.refs_3_), channel_id=1, source_target_pairs={{0,1},{1,0},{2,3},{3,2},{4,5},{5,4},{6,7},{7,6},{8,9},{9,8},{10,11... | collective-permute-start | bytes 368648 | tf_op jit(solution)/shard_map/ppermute | solution.py:27
  14.1 0.9 %copy-start.1 = (bf16[2,4,48,128]{3,2,1,0:T(8,128)(2,1)S(1)}, bf16[2,4,48,128]{3,2,1,0:T(8,128)(2,1)}, u32[]{:S(2)}) copy-start(bf16[2,4,48,128]{3,2,1,0:T(8,128)(2,1)} %refs_8_.1) | copy-start | bytes 294916
  16.0 11.6 %collective-permute-start.9 = (bf16[288,128]{1,0:T(8,128)(2,1)S(1)}, bf16[288,128]{1,0:T(8,128)(2,1)S(1)}, u32[]{:S(2)}, u32[]{:S(2)}) collective-permute-start(bf16[288,128]{1,0:T(8,128)(2,1)S(1)} %get-tuple-element.27), channel_id=1, source_target_pairs={{0,8},{1,9},{2,10},{3,11},{4,12},{5,13},{6,14},{7,15},{8,0},{9,1},... | collective-permute-start | bytes 221192 | tf_op jit(solution)/shard_map/ppermute | solution.py:27
  17.6 9.9 %collective-permute-start.10 = (bf16[288,128]{1,0:T(8,128)(2,1)S(1)}, bf16[288,128]{1,0:T(8,128)(2,1)S(1)}, u32[]{:S(2)}, u32[]{:S(2)}) collective-permute-start(bf16[288,128]{1,0:T(8,128)(2,1)S(1)} %get-tuple-element.28), channel_id=1, source_target_pairs={{8,16},{9,17},{10,18},{11,19},{12,20},{13,21},{14,22},{15,23},{16,... | collective-permute-start | bytes 221192 | tf_op jit(solution)/shard_map/ppermute | solution.py:27
  18.3 14.5 %collective-permute-start.7 = (bf16[192,128]{1,0:T(8,128)(2,1)S(1)}, bf16[192,128]{1,0:T(8,128)(2,1)S(1)}, u32[]{:S(2)}, u32[]{:S(2)}) collective-permute-start(bf16[192,128]{1,0:T(8,128)(2,1)S(1)} %get-tuple-element.25), channel_id=1, source_target_pairs={{4,8},{5,9},{6,10},{7,11},{8,4},{9,5},{10,6},{11,7},{12,16},{13,17... | collective-permute-start | bytes 147464 | tf_op jit(solution)/shard_map/ppermute | solution.py:27
  19.0 13.8 %collective-permute-start.8 = (bf16[192,128]{1,0:T(8,128)(2,1)S(1)}, bf16[192,128]{1,0:T(8,128)(2,1)S(1)}, u32[]{:S(2)}, u32[]{:S(2)}) collective-permute-start(bf16[192,128]{1,0:T(8,128)(2,1)S(1)} %get-tuple-element.26), channel_id=1, source_target_pairs={{0,4},{1,5},{2,6},{3,7},{4,0},{5,1},{6,2},{7,3},{8,12},{9,13},{10,... | collective-permute-start | bytes 147464 | tf_op jit(solution)/shard_map/ppermute | solution.py:27
  26.1 6.7 %copy-start = (bf16[27,128,128]{2,1,0:T(8,128)(2,1)S(1)}, bf16[27,128,128]{2,1,0:T(8,128)(2,1)}, u32[]{:S(2)}) copy-start(bf16[27,128,128]{2,1,0:T(8,128)(2,1)} %kernel_ref.1) | copy-start | bytes 2654212
  26.1 6.7 %copy-start.2 = (bf16[2,4,48,128]{3,2,1,0:T(8,128)(2,1)S(1)}, bf16[2,4,48,128]{3,2,1,0:T(8,128)(2,1)}, u32[]{:S(2)}) copy-start(bf16[2,4,48,128]{3,2,1,0:T(8,128)(2,1)} %inputs_ref.1) | copy-start | bytes 294916
  28.3 5.8 %collective-permute-start.11 = (bf16[112,128]{1,0:T(8,128)(2,1)S(1)}, bf16[112,128]{1,0:T(8,128)(2,1)S(1)}, u32[]{:S(2)}, u32[]{:S(2)}) collective-permute-start(bf16[112,128]{1,0:T(8,128)(2,1)S(1)} %get-tuple-element.35), channel_id=1, source_target_pairs={{0,8},{1,9},{2,10},{3,11},{4,12},{5,13},{6,14},{7,15},{8,0},{9,1},... | collective-permute-start | bytes 86024 | tf_op jit(solution)/shard_map/ppermute | solution.py:27
  28.4 5.8 %collective-permute-start.12 = (bf16[112,128]{1,0:T(8,128)(2,1)S(1)}, bf16[112,128]{1,0:T(8,128)(2,1)S(1)}, u32[]{:S(2)}, u32[]{:S(2)}) collective-permute-start(bf16[112,128]{1,0:T(8,128)(2,1)S(1)} %get-tuple-element.36), channel_id=1, source_target_pairs={{0,16},{1,17},{2,18},{3,19},{4,20},{5,21},{6,22},{7,23},{8,24},{9,... | collective-permute-start | bytes 86024 | tf_op jit(solution)/shard_map/ppermute | solution.py:27
  29.4 5.7 %collective-permute-start.13 = (bf16[112,128]{1,0:T(8,128)(2,1)S(1)}, bf16[112,128]{1,0:T(8,128)(2,1)S(1)}, u32[]{:S(2)}, u32[]{:S(2)}) collective-permute-start(bf16[112,128]{1,0:T(8,128)(2,1)S(1)} %get-tuple-element.37), channel_id=1, source_target_pairs={{0,24},{1,25},{2,26},{3,27},{4,28},{5,29},{6,30},{7,31},{8,16},{9,... | collective-permute-start | bytes 86024 | tf_op jit(solution)/shard_map/ppermute | solution.py:27
where the time goes:
time: 36.1 us; the launch traced here: 35.9 us
  starting transfers between devices  19.7 us (55%)
  waiting for transfers between devices  7.85 us (22%)
  Pallas kernels  5.4 us (15%)
  local copies, waits for them, and re-layouts  2.23 us (6%)
  between operations  0.73 us (2%)
    ppermute x14, starting transfers between devices, move(): return lax.ppermute(array, AXES, pairs)  19.7 us
    ppermute x14, waiting for transfers between devices, move(): return lax.ppermute(array, AXES, pairs)  7.85 us
    pallas_call x6, Pallas kernels, call(): return run(*args)  5.4 us
    unnamed x8, local copies, waits for them, and re-layouts  2.23 us
  transfers between devices with their start and end apart: 14, of which 5 were waited for; matrix products, arithmetic and copies ran while one was open for 2% of the time, Pallas kernels for 8%

commit v1 on v0

--- a/solution.py
+++ b/solution.py
@@ -41,11 +41,11 @@
     return found
 
 
-def call(body, outs, args, scratch=(), flops=0, moved=0, fetch=False):
+def call(body, outs, args, scratch=(), flops=0, moved=0, fetch=False, last=False):
     vmem = pl.BlockSpec(memory_space=pltpu.VMEM)
     run = pl.pallas_call(
         body,
-        out_shape=tuple(pltpu.VMEM(s, d) for s, d in outs),
+        out_shape=tuple((jax.ShapeDtypeStruct if last else pltpu.VMEM)(s, d) for s, d in outs),
         in_specs=[pl.BlockSpec(memory_space=pltpu.HBM) if fetch else vmem] * len(args),
         out_specs=tuple(vmem for _ in outs),
         scratch_shapes=list(scratch),
@@ -112,12 +112,63 @@
     return jnp.where(keep, moved, 0.0).astype(BF16)
 
 
-def unpack_body(dims, *refs):
+def edges_body(dims, *refs):
     _, parts_y, wx, wy, depth, chans = dims
     hi, lo, chip, core = spot()
     chips, half, block_o = parts_y // 2, chans // 2, chans // parts_y
+    blocks, outs = refs[: 4 * chips], refs[4 * chips :]
+    swapped = blocks[2 * chips :]
+    strip, quarter = wy * depth, parts_y // 4
+    rows, size = wx * strip, quarter * strip
+    lane = lax.broadcasted_iota(jnp.int32, (1, chans), 1)
+    far_row = pl.multiple_of(rows + (1 - lo) * (wx - 1) * depth, depth)
+    for out in outs:
+        out[size : size + depth] = swapped[chips][pl.ds(far_row, depth)]
+        out[size + depth :] = jnp.zeros((depth, chans), BF16)
+    for flip in near_flips(chips):
+
+        @pl.when((chip ^ flip) == chip + 2 * core - 1)
+        def _(flip=flip):
+            for out in outs:
+                out[size + depth :] = swapped[chips + flip][pl.ds(far_row, depth)]
+
+    for flip_lo in range(2):
+        from_lo = lo ^ flip_lo
+        row = pl.multiple_of(from_lo * (wx - 1) * strip, strip)
+        pieces = {}
+        for flip_core in range(2):
+            for flip in range(chips):
+                block = blocks[(2 * flip_core + flip_lo) * chips + flip]
+                from_y = 2 * (chip ^ flip) + (core ^ flip_core)
+                slot = from_y // quarter
+                value = block[pl.ds(row, strip)].astype(F32)
+                moved = pltpu.roll(value, (slot - flip_core) * block_o + half, 1)
+                keep = (lane >= slot * block_o) & (lane < (slot + 1) * block_o)
+                pieces[flip_core, flip] = (jnp.where(keep, moved, 0.0), from_y % quarter)
+        if quarter == 1:
+            total = sum(p for p, _ in list(pieces.values())[1:]) + list(pieces.values())[0][0]
+            totals = [(0, total)]
+        else:
+            totals = []
+            for n in range(quarter):
+                total = jnp.zeros((strip, chans), F32)
+                for piece, place in pieces.values():
+                    total = total + jnp.where(place == n, piece, 0.0)
+                totals.append((n, total))
+        for out, parity in zip(outs, (1, 0)):
+
+            @pl.when((hi + from_lo) % 2 == parity)
+            def _(out=out):
+                for n, total in totals:
+                    out[n * strip : (n + 1) * strip] = total.astype(BF16)
+
+
+def unpack_body(dims, *refs):
+    _, parts_y, wx, wy, depth, chans = dims
+    _, lo, chip, core = spot()
+    chips, half, block_o = parts_y // 2, chans // 2, chans // parts_y
     blocks, cot_ref = refs[: 4 * chips], refs[4 * chips]
-    acts, wide, even, odd, pad, cots = refs[4 * chips + 1 :]
+    acts, wide, pad, cots = refs[4 * chips + 1 :]
     rows = wx * wy * depth
     total_y, strip = wy * parts_y, wy * depth
     lane = lax.broadcasted_iota(jnp.int32, (1, chans), 1)
@@ -131,13 +182,8 @@
     swapped = blocks[2 * chips :]
     pad[1 : wx + 1, 1 : wy + 1] = cot_ref[...]
     near_row = pl.multiple_of(rows + lo * (wx - 1) * depth, depth)
-    far_row = pl.multiple_of(rows + (1 - lo) * (wx - 1) * depth, depth)
-    size = total_y // 4 * depth
     pad[facing, toward] = swapped[chips][pl.ds(near_row, depth)]
     pad[facing, away] = blank
-    for out in (even, odd):
-        out[size : size + depth] = swapped[chips][pl.ds(far_row, depth)]
-        out[size + depth :] = blank
     for x in range(wx):
         pad[x + 1, toward] = swapped[0][rows + x * depth : rows + (x + 1) * depth]
         pad[x + 1, away] = blank
@@ -146,8 +192,6 @@
         @pl.when((chip ^ flip) == chip + 2 * core - 1)
         def _(flip=flip):
             pad[facing, away] = swapped[chips + flip][pl.ds(near_row, depth)]
-            for out in (even, odd):
-                out[size + depth :] = swapped[chips + flip][pl.ds(far_row, depth)]
             for x in range(wx):
                 pad[x + 1, away] = swapped[flip][rows + x * depth : rows + (x + 1) * depth]
 
@@ -177,13 +221,6 @@
         return carry
 
     lax.fori_loop(0, total_y, merge, 0, unroll=4)
-    part_y = total_y // 4
-    for out, x in ((even, (1 - hi % 2) * (2 * wx - 1)), (odd, (hi % 2) * (2 * wx - 1))):
-        total = cots[0, x, 1 : 1 + part_y] + cots[1, x, 1 + part_y : 1 + 2 * part_y]
-        total = total + cots[2, x, 1 + 2 * part_y : 1 + 3 * part_y]
-        last = cots[0, x, 1 + 3 * part_y : 1 + 4 * part_y].reshape(size, chans).astype(F32)
-        last = pltpu.roll(last, 3 * block_o, 1).astype(BF16)
-        out[:size] = total.reshape(size, chans) + last
 
 
 def main_body(dims, acts, wide, sums, low, high):
@@ -367,13 +404,16 @@
     outer = move(outer, pairs_along(parts_x, parts_y, size, True))
     inner = move(inner, pairs_along(parts_x, parts_y, size, False))
 
-    acts, wide, end_even, end_odd, pad = call(
+    end_even, end_odd = call(
+        functools.partial(edges_body, dims),
+        [(((total_y // 4 + 2) * depth, chans), BF16)] * 2,
+        (*same, *other),
+    )
+    acts, wide, pad = call(
         functools.partial(unpack_body, dims),
         [
             ((total_x, total_y, depth, chans), BF16),
             ((total_x + 2, total_y, depth, chans), BF16),
-            (((total_y // 4 + 2) * depth, chans), BF16),
-            (((total_y // 4 + 2) * depth, chans), BF16),
             ((wx + 2, wy + 2, depth, chans), BF16),
         ],
         (*same, *other, cotangent),
@@ -415,6 +455,7 @@
         [((27, block_i, chans // parts_y), F32)],
         terms,
         moved=4 * his * 7 * block_i * chans,
+        last=True,
     )
     return (input_grad, kernel_grad)
 

time: 36.1 us -> 35.4 us (0.981)
  local copies, waits for them, and re-layouts: 2.23 us -> 0.66 us
  Pallas kernels: 5.4 us -> 6.28 us
    unnamed x8 -> x7, local copies, waits for them, and re-layouts: 2.23 us -> 0.66 us
    pallas_call x6 -> x7, Pallas kernels: 5.4 us -> 6.28 us  [call(): return run(*args)]
  transfers between devices with their start and end apart: 14 -> 14, of which waited for: 5 -> 5; matrix products, arithmetic and copies ran while one was open for 2% -> 2% of each run, Pallas kernels for 8% -> 11%
where the time goes in v1:
time: 35.4 us; the launch traced here: 35.2 us
  starting transfers between devices  19.7 us (56%)
  waiting for transfers between devices  7.84 us (22%)
  Pallas kernels  6.28 us (18%)
  between operations  0.75 us (2%)
  local copies, waits for them, and re-layouts  0.66 us (2%)
    ppermute x14, starting transfers between devices, move(): return lax.ppermute(array, AXES, pairs)  19.7 us
    ppermute x14, waiting for transfers between devices, move(): return lax.ppermute(array, AXES, pairs)  7.84 us
    pallas_call x7, Pallas kernels, call(): return run(*args)  6.28 us
  transfers between devices with their start and end apart: 14, of which 5 were waited for; matrix products, arithmetic and copies ran while one was open for 2% of the time, Pallas kernels for 11%

profile of v1, /device:TPU:0, one launch (start us, length us, event | category | flops | bytes accessed | tf_op | source)
XLA Modules:
  0.0 35.2 jit_solution(4696756255375633653)
XLA Ops:
  0.6 1.4 %shard_map.50 = (bf16[480,128]{1,0:T(8,128)(2,1)S(1)}, bf16[480,128]{1,0:T(8,128)(2,1)S(1)}, bf16[480,128]{1,0:T(8,128)(2,1)S(1)}, bf16[480,128]{1,0:T(8,128)(2,...) custom-call(bf16[2,4,48,128]{3,2,1,0:T(8,128)(2,1)} %inputs_ref.1, bf16[2,4,48,128]{3,2,1,0:T(8,128)(2,1)} %refs_8_.1), custom_call_target="tpu_custom_call" | custom-call | flops 100663296 | bytes 688128 | tf_op jit(solution)/shard_map/pallas_call | solution.py:57
  2.0 3.0 %collective-permute-start = (bf16[480,128]{1,0:T(8,128)(2,1)S(1)}, bf16[480,128]{1,0:T(8,128)(2,1)S(1)}, u32[]{:S(2)}, u32[]{:S(2)}) collective-permute-start(bf16[480,128]{1,0:T(8,128)(2,1)S(1)} %get-tuple-element.21), channel_id=1, source_target_pairs={{0,2},{1,3},{2,0},{3,1},{4,6},{5,7},{6,4},{7,5},{8,10},{9,11},{10,... | collective-permute-start | bytes 368648 | tf_op jit(solution)/shard_map/ppermute | solution.py:27
  5.1 1.5 %collective-permute-start.1 = (bf16[480,128]{1,0:T(8,128)(2,1)S(1)}, bf16[480,128]{1,0:T(8,128)(2,1)S(1)}, u32[]{:S(2)}, u32[]{:S(2)}) collective-permute-start(bf16[480,128]{1,0:T(8,128)(2,1)S(1)} %get-tuple-element.22), channel_id=1, source_target_pairs={{0,4},{1,5},{2,6},{3,7},{4,0},{5,1},{6,2},{7,3},{8,12},{9,13},{10,... | collective-permute-start | bytes 368648 | tf_op jit(solution)/shard_map/ppermute | solution.py:27
  6.6 0.0 collective-permute-start.2
  6.6 0.0 collective-permute-start.3
  6.6 2.2 %collective-permute-done.refs_1_ = bf16[480,128]{1,0:T(8,128)(2,1)S(1)} collective-permute-done((bf16[480,128]{1,0:T(8,128)(2,1)S(1)}, bf16[480,128]{1,0:T(8,128)(2,1)S(1)}, u32[]{:S(2)}, u32[]{:S(2)}) %collective-permute-start) | collective-permute-done | bytes 122912 | tf_op jit(solution)/shard_map/ppermute | solution.py:27
  8.8 0.0 collective-permute-start.4
  8.8 3.8 %collective-permute-done.1.refs_2_ = bf16[480,128]{1,0:T(8,128)(2,1)S(1)} collective-permute-done((bf16[480,128]{1,0:T(8,128)(2,1)S(1)}, bf16[480,128]{1,0:T(8,128)(2,1)S(1)}, u32[]{:S(2)}, u32[]{:S(2)}) %collective-permute-start.1) | collective-permute-done | bytes 122912 | tf_op jit(solution)/shard_map/ppermute | solution.py:27
  12.6 0.0 collective-permute-start.5
  12.6 0.0 collective-permute-done.2.refs_3_
  12.6 0.5 %collective-permute-start.6 = (bf16[480,128]{1,0:T(8,128)(2,1)S(1)}, bf16[480,128]{1,0:T(8,128)(2,1)S(1)}, u32[]{:S(2)}, u32[]{:S(2)}) collective-permute-start(bf16[480,128]{1,0:T(8,128)(2,1)S(1)} %collective-permute-done.2.refs_3_), channel_id=1, source_target_pairs={{0,1},{1,0},{2,3},{3,2},{4,5},{5,4},{6,7},{7,6},{8,9},{9,8},{10,11... | collective-permute-start | bytes 368648 | tf_op jit(solution)/shard_map/ppermute | solution.py:27
  13.1 0.0 collective-permute-done.3.refs_4_
  13.1 0.0 collective-permute-done.4.refs_5_
  13.1 0.8 %collective-permute-done.5.refs_6_ = bf16[480,128]{1,0:T(8,128)(2,1)S(1)} collective-permute-done((bf16[480,128]{1,0:T(8,128)(2,1)S(1)}, bf16[480,128]{1,0:T(8,128)(2,1)S(1)}, u32[]{:S(2)}, u32[]{:S(2)}) %collective-permute-start.5) | collective-permute-done | bytes 122912 | tf_op jit(solution)/shard_map/ppermute | solution.py:27
  13.9 0.2 collective-permute-done.6.refs_7_
  14.1 0.3 shard_map.52
  14.4 1.6 %collective-permute-start.9 = (bf16[288,128]{1,0:T(8,128)(2,1)S(1)}, bf16[288,128]{1,0:T(8,128)(2,1)S(1)}, u32[]{:S(2)}, u32[]{:S(2)}) collective-permute-start(bf16[288,128]{1,0:T(8,128)(2,1)S(1)} %get-tuple-element.27), channel_id=1, source_target_pairs={{0,8},{1,9},{2,10},{3,11},{4,12},{5,13},{6,14},{7,15},{8,0},{9,1},... | collective-permute-start | bytes 221192 | tf_op jit(solution)/shard_map/ppermute | solution.py:27
  16.0 0.7 %collective-permute-start.10 = (bf16[288,128]{1,0:T(8,128)(2,1)S(1)}, bf16[288,128]{1,0:T(8,128)(2,1)S(1)}, u32[]{:S(2)}, u32[]{:S(2)}) collective-permute-start(bf16[288,128]{1,0:T(8,128)(2,1)S(1)} %get-tuple-element.28), channel_id=1, source_target_pairs={{8,16},{9,17},{10,18},{11,19},{12,20},{13,21},{14,22},{15,23},{16,... | collective-permute-start | bytes 221192 | tf_op jit(solution)/shard_map/ppermute | solution.py:27
  16.7 0.7 %collective-permute-start.7 = (bf16[192,128]{1,0:T(8,128)(2,1)S(1)}, bf16[192,128]{1,0:T(8,128)(2,1)S(1)}, u32[]{:S(2)}, u32[]{:S(2)}) collective-permute-start(bf16[192,128]{1,0:T(8,128)(2,1)S(1)} %get-tuple-element.25), channel_id=1, source_target_pairs={{4,8},{5,9},{6,10},{7,11},{8,4},{9,5},{10,6},{11,7},{12,16},{13,17... | collective-permute-start | bytes 147464 | tf_op jit(solution)/shard_map/ppermute | solution.py:27
  17.3 7.2 %collective-permute-start.8 = (bf16[192,128]{1,0:T(8,128)(2,1)S(1)}, bf16[192,128]{1,0:T(8,128)(2,1)S(1)}, u32[]{:S(2)}, u32[]{:S(2)}) collective-permute-start(bf16[192,128]{1,0:T(8,128)(2,1)S(1)} %get-tuple-element.26), channel_id=1, source_target_pairs={{0,4},{1,5},{2,6},{3,7},{4,0},{5,1},{6,2},{7,3},{8,12},{9,13},{10,... | collective-permute-start | bytes 147464 | tf_op jit(solution)/shard_map/ppermute | solution.py:27
  24.5 0.9 %shard_map.51 = (bf16[4,16,48,128]{3,2,1,0:T(8,128)(2,1)S(1)}, bf16[6,16,48,128]{3,2,1,0:T(8,128)(2,1)S(1)}, bf16[4,6,48,128]{3,2,1,0:T(8,128)(2,1)S(1)}) custom-call(bf16[480,128]{1,0:T(8,128)(2,1)S(1)} %get-tuple-element.20.refs_0_, bf16[480,128]{1,0:T(8,128)(2,1)S(1)} %collective-permute-done.refs_1_, ...), custom_call_target="tpu_custom_call" | custom-call | bytes 786432 | tf_op jit(solution)/shard_map/pallas_call | solution.py:57
  25.5 0.0 copy-start
  25.5 0.0 copy-start.2
  25.5 1.4 %shard_map.54 = (f32[192,384]{1,0:T(8,128)S(1)}, bf16[768,192]{1,0:T(8,128)(2,1)S(1)}, bf16[768,192]{1,0:T(8,128)(2,1)S(1)}) custom-call(bf16[4,16,48,128]{3,2,1,0:T(8,128)(2,1)S(1)} %get-tuple-element.29.acts, bf16[6,16,48,128]{3,2,1,0:T(8,128)(2,1)S(1)} %get-tuple-element.30.wide), custom_call_target="tpu_custom_call" | custom-call | flops 452984832 | bytes 786432 | tf_op jit(solution)/shard_map/pallas_call | solution.py:57
  26.9 0.7 %shard_map.55 = (f32[112,128]{1,0:T(8,128)S(1)}, bf16[112,128]{1,0:T(8,128)(2,1)S(1)}, bf16[112,128]{1,0:T(8,128)(2,1)S(1)}, bf16[112,128]{1,0:T(8,128)(2,1)S(1)}) custom-call(f32[192,384]{1,0:T(8,128)S(1)} %get-tuple-element.31.main_ref, bf16[768,192]{1,0:T(8,128)(2,1)S(1)} %get-tuple-element.32.low, bf16[768,192]{1,0:T(8,128)(2,1)S(1)} %get-tuple-element.33.high, ...), custom_call_target="tpu_custom_call" | custom-call | flops 75497472 | bytes 393216 | tf_op jit(solution)/shard_map/pallas_call | solution.py:57
  27.7 0.1 collective-permute-start.11
  27.8 1.0 %collective-permute-start.12 = (bf16[112,128]{1,0:T(8,128)(2,1)S(1)}, bf16[112,128]{1,0:T(8,128)(2,1)S(1)}, u32[]{:S(2)}, u32[]{:S(2)}) collective-permute-start(bf16[112,128]{1,0:T(8,128)(2,1)S(1)} %get-tuple-element.36), channel_id=1, source_target_pairs={{0,16},{1,17},{2,18},{3,19},{4,20},{5,21},{6,22},{7,23},{8,24},{9,... | collective-permute-start | bytes 86024 | tf_op jit(solution)/shard_map/ppermute | solution.py:27
  28.7 3.4 %collective-permute-start.13 = (bf16[112,128]{1,0:T(8,128)(2,1)S(1)}, bf16[112,128]{1,0:T(8,128)(2,1)S(1)}, u32[]{:S(2)}, u32[]{:S(2)}) collective-permute-start(bf16[112,128]{1,0:T(8,128)(2,1)S(1)} %get-tuple-element.37), channel_id=1, source_target_pairs={{0,24},{1,25},{2,26},{3,27},{4,28},{5,29},{6,30},{7,31},{8,16},{9,... | collective-permute-start | bytes 86024 | tf_op jit(solution)/shard_map/ppermute | solution.py:27
  32.2 0.7 %shard_map.53 = bf16[2,4,48,128]{3,2,1,0:T(8,128)(2,1)S(1)} custom-call(bf16[2,4,48,128]{3,2,1,0:T(8,128)(2,1)S(1)} %copy-done.2, bf16[4,6,48,128]{3,2,1,0:T(8,128)(2,1)S(1)} %get-tuple-element.24.pad_ref, bf16[192,128]{1,0:T(8,128)(2,1)S(1)} %collective-permute-done.7.outer_ref, bf16[192,128]{1,0:T(8,128)(2,1)S(1)} %collective-permute-done.8.inner_ref, ...), custom_call_target="tpu_custom_call" | custom-call | flops 339738624 | bytes 884736 | tf_op jit(solution)/shard_map/pallas_call | solution.py:57
  32.9 0.6 %copy.5 = bf16[2,4,48,128]{3,2,1,0:T(8,128)(2,1)} copy(bf16[2,4,48,128]{3,2,1,0:T(8,128)(2,1)S(1)} %shard_map.53) | data formatting | bytes 196608
  33.5 0.9 %collective-permute-done.13.refs_3_ = bf16[112,128]{1,0:T(8,128)(2,1)S(1)} collective-permute-done((bf16[112,128]{1,0:T(8,128)(2,1)S(1)}, bf16[112,128]{1,0:T(8,128)(2,1)S(1)}, u32[]{:S(2)}, u32[]{:S(2)}) %collective-permute-start.13) | collective-permute-done | bytes 28704 | tf_op jit(solution)/shard_map/ppermute | solution.py:27
  34.4 0.8 %shard_map.56 = f32[27,16,32]{2,1,0:T(8,128)} custom-call(f32[112,128]{1,0:T(8,128)S(1)} %get-tuple-element.34.refs_0_, bf16[112,128]{1,0:T(8,128)(2,1)S(1)} %collective-permute-done.11.refs_1_, bf16[112,128]{1,0:T(8,128)(2,1)S(1)} %collective-permute-done.12.refs_2_, bf16[112,128]{1,0:T(8,128)(2,1)S(1)} %collective-permute-done.13.refs_3_), custom_call_target="tpu_custom_call" | custom-call | bytes 229376 | tf_op jit(solution)/shard_map/pallas_call | solution.py:57
  (10 shorter events, 0.0 us)
Async XLA Ops:
  0.6 23.9 %copy-start.1 = (bf16[2,4,48,128]{3,2,1,0:T(8,128)(2,1)S(1)}, bf16[2,4,48,128]{3,2,1,0:T(8,128)(2,1)}, u32[]{:S(2)}) copy-start(bf16[2,4,48,128]{3,2,1,0:T(8,128)(2,1)} %refs_8_.1) | copy-start | bytes 294916
  2.0 6.7 %collective-permute-start = (bf16[480,128]{1,0:T(8,128)(2,1)S(1)}, bf16[480,128]{1,0:T(8,128)(2,1)S(1)}, u32[]{:S(2)}, u32[]{:S(2)}) collective-permute-start(bf16[480,128]{1,0:T(8,128)(2,1)S(1)} %get-tuple-element.21), channel_id=1, source_target_pairs={{0,2},{1,3},{2,0},{3,1},{4,6},{5,7},{6,4},{7,5},{8,10},{9,11},{10,... | collective-permute-start | bytes 368648 | tf_op jit(solution)/shard_map/ppermute | solution.py:27
  5.1 7.5 %collective-permute-start.1 = (bf16[480,128]{1,0:T(8,128)(2,1)S(1)}, bf16[480,128]{1,0:T(8,128)(2,1)S(1)}, u32[]{:S(2)}, u32[]{:S(2)}) collective-permute-start(bf16[480,128]{1,0:T(8,128)(2,1)S(1)} %get-tuple-element.22), channel_id=1, source_target_pairs={{0,4},{1,5},{2,6},{3,7},{4,0},{5,1},{6,2},{7,3},{8,12},{9,13},{10,... | collective-permute-start | bytes 368648 | tf_op jit(solution)/shard_map/ppermute | solution.py:27
  6.6 6.0 %collective-permute-start.2 = (bf16[480,128]{1,0:T(8,128)(2,1)S(1)}, bf16[480,128]{1,0:T(8,128)(2,1)S(1)}, u32[]{:S(2)}, u32[]{:S(2)}) collective-permute-start(bf16[480,128]{1,0:T(8,128)(2,1)S(1)} %get-tuple-element.23), channel_id=1, source_target_pairs={{0,6},{1,7},{2,4},{3,5},{4,2},{5,3},{6,0},{7,1},{8,14},{9,15},{10,... | collective-permute-start | bytes 368648 | tf_op jit(solution)/shard_map/ppermute | solution.py:27
  6.6 6.5 %collective-permute-start.3 = (bf16[480,128]{1,0:T(8,128)(2,1)S(1)}, bf16[480,128]{1,0:T(8,128)(2,1)S(1)}, u32[]{:S(2)}, u32[]{:S(2)}) collective-permute-start(bf16[480,128]{1,0:T(8,128)(2,1)S(1)} %get-tuple-element.20.refs_0_), channel_id=1, source_target_pairs={{0,1},{1,0},{2,3},{3,2},{4,5},{5,4},{6,7},{7,6},{8,9},{9,8},{10,11... | collective-permute-start | bytes 368648 | tf_op jit(solution)/shard_map/ppermute | solution.py:27
  8.8 4.3 %collective-permute-start.4 = (bf16[480,128]{1,0:T(8,128)(2,1)S(1)}, bf16[480,128]{1,0:T(8,128)(2,1)S(1)}, u32[]{:S(2)}, u32[]{:S(2)}) collective-permute-start(bf16[480,128]{1,0:T(8,128)(2,1)S(1)} %collective-permute-done.refs_1_), channel_id=1, source_target_pairs={{0,1},{1,0},{2,3},{3,2},{4,5},{5,4},{6,7},{7,6},{8,9},{9,8},{10,11... | collective-permute-start | bytes 368648 | tf_op jit(solution)/shard_map/ppermute | solution.py:27
  12.6 1.3 %collective-permute-start.5 = (bf16[480,128]{1,0:T(8,128)(2,1)S(1)}, bf16[480,128]{1,0:T(8,128)(2,1)S(1)}, u32[]{:S(2)}, u32[]{:S(2)}) collective-permute-start(bf16[480,128]{1,0:T(8,128)(2,1)S(1)} %collective-permute-done.1.refs_2_), channel_id=1, source_target_pairs={{0,1},{1,0},{2,3},{3,2},{4,5},{5,4},{6,7},{7,6},{8,9},{9,8},{10,11... | collective-permute-start | bytes 368648 | tf_op jit(solution)/shard_map/ppermute | solution.py:27
  12.6 1.5 %collective-permute-start.6 = (bf16[480,128]{1,0:T(8,128)(2,1)S(1)}, bf16[480,128]{1,0:T(8,128)(2,1)S(1)}, u32[]{:S(2)}, u32[]{:S(2)}) collective-permute-start(bf16[480,128]{1,0:T(8,128)(2,1)S(1)} %collective-permute-done.2.refs_3_), channel_id=1, source_target_pairs={{0,1},{1,0},{2,3},{3,2},{4,5},{5,4},{6,7},{7,6},{8,9},{9,8},{10,11... | collective-permute-start | bytes 368648 | tf_op jit(solution)/shard_map/ppermute | solution.py:27
  14.4 12.6 %collective-permute-start.9 = (bf16[288,128]{1,0:T(8,128)(2,1)S(1)}, bf16[288,128]{1,0:T(8,128)(2,1)S(1)}, u32[]{:S(2)}, u32[]{:S(2)}) collective-permute-start(bf16[288,128]{1,0:T(8,128)(2,1)S(1)} %get-tuple-element.27), channel_id=1, source_target_pairs={{0,8},{1,9},{2,10},{3,11},{4,12},{5,13},{6,14},{7,15},{8,0},{9,1},... | collective-permute-start | bytes 221192 | tf_op jit(solution)/shard_map/ppermute | solution.py:27
  16.0 10.9 %collective-permute-start.10 = (bf16[288,128]{1,0:T(8,128)(2,1)S(1)}, bf16[288,128]{1,0:T(8,128)(2,1)S(1)}, u32[]{:S(2)}, u32[]{:S(2)}) collective-permute-start(bf16[288,128]{1,0:T(8,128)(2,1)S(1)} %get-tuple-element.28), channel_id=1, source_target_pairs={{8,16},{9,17},{10,18},{11,19},{12,20},{13,21},{14,22},{15,23},{16,... | collective-permute-start | bytes 221192 | tf_op jit(solution)/shard_map/ppermute | solution.py:27
  16.7 15.5 %collective-permute-start.7 = (bf16[192,128]{1,0:T(8,128)(2,1)S(1)}, bf16[192,128]{1,0:T(8,128)(2,1)S(1)}, u32[]{:S(2)}, u32[]{:S(2)}) collective-permute-start(bf16[192,128]{1,0:T(8,128)(2,1)S(1)} %get-tuple-element.25), channel_id=1, source_target_pairs={{4,8},{5,9},{6,10},{7,11},{8,4},{9,5},{10,6},{11,7},{12,16},{13,17... | collective-permute-start | bytes 147464 | tf_op jit(solution)/shard_map/ppermute | solution.py:27
  17.3 14.8 %collective-permute-start.8 = (bf16[192,128]{1,0:T(8,128)(2,1)S(1)}, bf16[192,128]{1,0:T(8,128)(2,1)S(1)}, u32[]{:S(2)}, u32[]{:S(2)}) collective-permute-start(bf16[192,128]{1,0:T(8,128)(2,1)S(1)} %get-tuple-element.26), channel_id=1, source_target_pairs={{0,4},{1,5},{2,6},{3,7},{4,0},{5,1},{6,2},{7,3},{8,12},{9,13},{10,... | collective-permute-start | bytes 147464 | tf_op jit(solution)/shard_map/ppermute | solution.py:27
  25.5 6.7 %copy-start = (bf16[27,128,128]{2,1,0:T(8,128)(2,1)S(1)}, bf16[27,128,128]{2,1,0:T(8,128)(2,1)}, u32[]{:S(2)}) copy-start(bf16[27,128,128]{2,1,0:T(8,128)(2,1)} %kernel_ref.1) | copy-start | bytes 2654212
  25.5 6.7 %copy-start.2 = (bf16[2,4,48,128]{3,2,1,0:T(8,128)(2,1)S(1)}, bf16[2,4,48,128]{3,2,1,0:T(8,128)(2,1)}, u32[]{:S(2)}) copy-start(bf16[2,4,48,128]{3,2,1,0:T(8,128)(2,1)} %inputs_ref.1) | copy-start | bytes 294916
  27.7 5.8 %collective-permute-start.11 = (bf16[112,128]{1,0:T(8,128)(2,1)S(1)}, bf16[112,128]{1,0:T(8,128)(2,1)S(1)}, u32[]{:S(2)}, u32[]{:S(2)}) collective-permute-start(bf16[112,128]{1,0:T(8,128)(2,1)S(1)} %get-tuple-element.35), channel_id=1, source_target_pairs={{0,8},{1,9},{2,10},{3,11},{4,12},{5,13},{6,14},{7,15},{8,0},{9,1},... | collective-permute-start | bytes 86024 | tf_op jit(solution)/shard_map/ppermute | solution.py:27
  27.8 5.8 %collective-permute-start.12 = (bf16[112,128]{1,0:T(8,128)(2,1)S(1)}, bf16[112,128]{1,0:T(8,128)(2,1)S(1)}, u32[]{:S(2)}, u32[]{:S(2)}) collective-permute-start(bf16[112,128]{1,0:T(8,128)(2,1)S(1)} %get-tuple-element.36), channel_id=1, source_target_pairs={{0,16},{1,17},{2,18},{3,19},{4,20},{5,21},{6,22},{7,23},{8,24},{9,... | collective-permute-start | bytes 86024 | tf_op jit(solution)/shard_map/ppermute | solution.py:27
  28.7 5.7 %collective-permute-start.13 = (bf16[112,128]{1,0:T(8,128)(2,1)S(1)}, bf16[112,128]{1,0:T(8,128)(2,1)S(1)}, u32[]{:S(2)}, u32[]{:S(2)}) collective-permute-start(bf16[112,128]{1,0:T(8,128)(2,1)S(1)} %get-tuple-element.37), channel_id=1, source_target_pairs={{0,24},{1,25},{2,26},{3,27},{4,28},{5,29},{6,30},{7,31},{8,16},{9,... | collective-permute-start | bytes 86024 | tf_op jit(solution)/shard_map/ppermute | solution.py:27

commit v2 on v1

--- a/solution.py
+++ b/solution.py
@@ -36,8 +36,7 @@
     for i in range(size):
         at = (i // stride) % count
         to = at ^ 1 if not odd else (at - 1 if at % 2 == 0 else at + 1)
-        if 0 <= to < count:
-            found.append((i, i + (to - at) * stride))
+        found.append((i, i + (to - at) * stride if 0 <= to < count else i ^ 1))
     return found
 
 
@@ -272,7 +271,8 @@
             cots[end, slot, 0] = blank
             cots[end, slot, total_y + 1] = blank
     for ref, end in ((even, 1 - hi % 2), (odd, hi % 2)):
-        value = ref[:size].astype(F32)
+        inside = jnp.where(end == 1, hi < his - 1, hi > 0)
+        value = jnp.where(inside, ref[:size].astype(F32), 0.0)
         for slot in range(3):
             for part in range(4):
                 cots[end, slot, 1 + part * part_y : 1 + (part + 1) * part_y] = in_lanes(
@@ -309,7 +309,7 @@
 
 
 def back_body(dims, inputs_ref, pad_ref, outer_ref, inner_ref, even, odd, kernel_ref, out_ref, pad):
-    _, parts_y, wx, wy, depth, chans = dims
+    parts_x, parts_y, wx, wy, depth, chans = dims
     hi, lo, _, core = spot()
     rows = wx * wy * depth
     pad[...] = pad_ref[...]
@@ -323,6 +323,10 @@
         def _(ref=ref):
             pad[lo * (wx + 1), toward] = ref[size : size + depth]
             pad[lo * (wx + 1), away] = ref[size + depth :]
+
+    @pl.when(jnp.where(lo == 0, hi == 0, hi == parts_x // 2 - 1))
+    def _():
+        pad[lo * (wx + 1)] = jnp.zeros((wy + 2, depth, chans), BF16)
 
     left, right = [], []
     for jx in range(3):

time: 35.4 us -> 31.5 us (0.89)
  starting transfers between devices: 19.7 us -> 15.8 us
    ppermute x14, starting transfers between devices: 19.7 us -> 15.8 us  [move(): return lax.ppermute(array, AXES, pairs)]
  transfers between devices with their start and end apart: 14 -> 14, of which waited for: 5 -> 5; matrix products, arithmetic and copies ran while one was open for 2% -> 2% of each run, Pallas kernels for 11% -> 12%
where the time goes in v2:
time: 31.5 us; the launch traced here: 31.3 us
  starting transfers between devices  15.8 us (50%)
  waiting for transfers between devices  7.82 us (25%)
  Pallas kernels  6.34 us (20%)
  between operations  0.74 us (2%)
  local copies, waits for them, and re-layouts  0.66 us (2%)
    ppermute x14, starting transfers between devices, move(): return lax.ppermute(array, AXES, pairs)  15.8 us
    ppermute x14, waiting for transfers between devices, move(): return lax.ppermute(array, AXES, pairs)  7.82 us
    pallas_call x7, Pallas kernels, call(): return run(*args)  6.34 us
    unnamed x7, local copies, waits for them, and re-layouts  0.66 us
  transfers between devices with their start and end apart: 14, of which 5 were waited for; matrix products, arithmetic and copies ran while one was open for 2% of the time, Pallas kernels for 12%

profile of v2, /device:TPU:0, one launch (start us, length us, event | category | flops | bytes accessed | tf_op | source)
XLA Modules:
  0.0 31.3 jit_solution(18182921202799708293)
XLA Ops:
  0.6 1.4 %shard_map.50 = (bf16[480,128]{1,0:T(8,128)(2,1)S(1)}, bf16[480,128]{1,0:T(8,128)(2,1)S(1)}, bf16[480,128]{1,0:T(8,128)(2,1)S(1)}, bf16[480,128]{1,0:T(8,128)(2,...) custom-call(bf16[2,4,48,128]{3,2,1,0:T(8,128)(2,1)} %inputs_ref.1, bf16[2,4,48,128]{3,2,1,0:T(8,128)(2,1)} %refs_8_.1), custom_call_target="tpu_custom_call" | custom-call | flops 100663296 | bytes 688128 | tf_op jit(solution)/shard_map/pallas_call | solution.py:56
  2.0 3.0 %collective-permute-start = (bf16[480,128]{1,0:T(8,128)(2,1)S(1)}, bf16[480,128]{1,0:T(8,128)(2,1)S(1)}, u32[]{:S(2)}, u32[]{:S(2)}) collective-permute-start(bf16[480,128]{1,0:T(8,128)(2,1)S(1)} %get-tuple-element.21), channel_id=1, source_target_pairs={{0,2},{1,3},{2,0},{3,1},{4,6},{5,7},{6,4},{7,5},{8,10},{9,11},{10,... | collective-permute-start | bytes 368648 | tf_op jit(solution)/shard_map/ppermute | solution.py:27
  5.1 1.5 %collective-permute-start.1 = (bf16[480,128]{1,0:T(8,128)(2,1)S(1)}, bf16[480,128]{1,0:T(8,128)(2,1)S(1)}, u32[]{:S(2)}, u32[]{:S(2)}) collective-permute-start(bf16[480,128]{1,0:T(8,128)(2,1)S(1)} %get-tuple-element.22), channel_id=1, source_target_pairs={{0,4},{1,5},{2,6},{3,7},{4,0},{5,1},{6,2},{7,3},{8,12},{9,13},{10,... | collective-permute-start | bytes 368648 | tf_op jit(solution)/shard_map/ppermute | solution.py:27
  6.6 0.0 collective-permute-start.2
  6.6 0.0 collective-permute-start.3
  6.6 2.2 %collective-permute-done.refs_1_ = bf16[480,128]{1,0:T(8,128)(2,1)S(1)} collective-permute-done((bf16[480,128]{1,0:T(8,128)(2,1)S(1)}, bf16[480,128]{1,0:T(8,128)(2,1)S(1)}, u32[]{:S(2)}, u32[]{:S(2)}) %collective-permute-start) | collective-permute-done | bytes 122912 | tf_op jit(solution)/shard_map/ppermute | solution.py:27
  8.8 0.0 collective-permute-start.4
  8.8 3.8 %collective-permute-done.1.refs_2_ = bf16[480,128]{1,0:T(8,128)(2,1)S(1)} collective-permute-done((bf16[480,128]{1,0:T(8,128)(2,1)S(1)}, bf16[480,128]{1,0:T(8,128)(2,1)S(1)}, u32[]{:S(2)}, u32[]{:S(2)}) %collective-permute-start.1) | collective-permute-done | bytes 122912 | tf_op jit(solution)/shard_map/ppermute | solution.py:27
  12.6 0.0 collective-permute-start.5
  12.6 0.0 collective-permute-done.2.refs_3_
  12.6 0.5 %collective-permute-start.6 = (bf16[480,128]{1,0:T(8,128)(2,1)S(1)}, bf16[480,128]{1,0:T(8,128)(2,1)S(1)}, u32[]{:S(2)}, u32[]{:S(2)}) collective-permute-start(bf16[480,128]{1,0:T(8,128)(2,1)S(1)} %collective-permute-done.2.refs_3_), channel_id=1, source_target_pairs={{0,1},{1,0},{2,3},{3,2},{4,5},{5,4},{6,7},{7,6},{8,9},{9,8},{10,11... | collective-permute-start | bytes 368648 | tf_op jit(solution)/shard_map/ppermute | solution.py:27
  13.1 0.0 collective-permute-done.3.refs_4_
  13.1 0.0 collective-permute-done.4.refs_5_
  13.1 0.8 %collective-permute-done.5.refs_6_ = bf16[480,128]{1,0:T(8,128)(2,1)S(1)} collective-permute-done((bf16[480,128]{1,0:T(8,128)(2,1)S(1)}, bf16[480,128]{1,0:T(8,128)(2,1)S(1)}, u32[]{:S(2)}, u32[]{:S(2)}) %collective-permute-start.5) | collective-permute-done | bytes 122912 | tf_op jit(solution)/shard_map/ppermute | solution.py:27
  13.9 0.2 collective-permute-done.6.refs_7_
  14.1 0.3 shard_map.52
  14.4 1.6 %collective-permute-start.9 = (bf16[288,128]{1,0:T(8,128)(2,1)S(1)}, bf16[288,128]{1,0:T(8,128)(2,1)S(1)}, u32[]{:S(2)}, u32[]{:S(2)}) collective-permute-start(bf16[288,128]{1,0:T(8,128)(2,1)S(1)} %get-tuple-element.27), channel_id=1, source_target_pairs={{0,8},{1,9},{2,10},{3,11},{4,12},{5,13},{6,14},{7,15},{8,0},{9,1},... | collective-permute-start | bytes 221192 | tf_op jit(solution)/shard_map/ppermute | solution.py:27
  16.0 0.1 collective-permute-start.10
  16.1 0.4 %collective-permute-start.7 = (bf16[192,128]{1,0:T(8,128)(2,1)S(1)}, bf16[192,128]{1,0:T(8,128)(2,1)S(1)}, u32[]{:S(2)}, u32[]{:S(2)}) collective-permute-start(bf16[192,128]{1,0:T(8,128)(2,1)S(1)} %get-tuple-element.25), channel_id=1, source_target_pairs={{0,1},{1,0},{2,3},{3,2},{4,8},{5,9},{6,10},{7,11},{8,4},{9,5},{10,... | collective-permute-start | bytes 147464 | tf_op jit(solution)/shard_map/ppermute | solution.py:27
  16.5 4.1 %collective-permute-start.8 = (bf16[192,128]{1,0:T(8,128)(2,1)S(1)}, bf16[192,128]{1,0:T(8,128)(2,1)S(1)}, u32[]{:S(2)}, u32[]{:S(2)}) collective-permute-start(bf16[192,128]{1,0:T(8,128)(2,1)S(1)} %get-tuple-element.26), channel_id=1, source_target_pairs={{0,4},{1,5},{2,6},{3,7},{4,0},{5,1},{6,2},{7,3},{8,12},{9,13},{10,... | collective-permute-start | bytes 147464 | tf_op jit(solution)/shard_map/ppermute | solution.py:27
  20.6 0.9 %shard_map.51 = (bf16[4,16,48,128]{3,2,1,0:T(8,128)(2,1)S(1)}, bf16[6,16,48,128]{3,2,1,0:T(8,128)(2,1)S(1)}, bf16[4,6,48,128]{3,2,1,0:T(8,128)(2,1)S(1)}) custom-call(bf16[480,128]{1,0:T(8,128)(2,1)S(1)} %get-tuple-element.20.refs_0_, bf16[480,128]{1,0:T(8,128)(2,1)S(1)} %collective-permute-done.refs_1_, ...), custom_call_target="tpu_custom_call" | custom-call | bytes 786432 | tf_op jit(solution)/shard_map/pallas_call | solution.py:56
  21.6 0.0 copy-start
  21.6 0.0 copy-start.2
  21.6 1.4 %shard_map.54 = (f32[192,384]{1,0:T(8,128)S(1)}, bf16[768,192]{1,0:T(8,128)(2,1)S(1)}, bf16[768,192]{1,0:T(8,128)(2,1)S(1)}) custom-call(bf16[4,16,48,128]{3,2,1,0:T(8,128)(2,1)S(1)} %get-tuple-element.29.acts, bf16[6,16,48,128]{3,2,1,0:T(8,128)(2,1)S(1)} %get-tuple-element.30.wide), custom_call_target="tpu_custom_call" | custom-call | flops 452984832 | bytes 786432 | tf_op jit(solution)/shard_map/pallas_call | solution.py:56
  23.1 0.8 %shard_map.55 = (f32[112,128]{1,0:T(8,128)S(1)}, bf16[112,128]{1,0:T(8,128)(2,1)S(1)}, bf16[112,128]{1,0:T(8,128)(2,1)S(1)}, bf16[112,128]{1,0:T(8,128)(2,1)S(1)}) custom-call(f32[192,384]{1,0:T(8,128)S(1)} %get-tuple-element.31.main_ref, bf16[768,192]{1,0:T(8,128)(2,1)S(1)} %get-tuple-element.32.low, bf16[768,192]{1,0:T(8,128)(2,1)S(1)} %get-tuple-element.33.high, ...), custom_call_target="tpu_custom_call" | custom-call | flops 75497472 | bytes 393216 | tf_op jit(solution)/shard_map/pallas_call | solution.py:56
  23.8 0.1 collective-permute-start.11
  23.9 0.9 %collective-permute-start.12 = (bf16[112,128]{1,0:T(8,128)(2,1)S(1)}, bf16[112,128]{1,0:T(8,128)(2,1)S(1)}, u32[]{:S(2)}, u32[]{:S(2)}) collective-permute-start(bf16[112,128]{1,0:T(8,128)(2,1)S(1)} %get-tuple-element.36), channel_id=1, source_target_pairs={{0,16},{1,17},{2,18},{3,19},{4,20},{5,21},{6,22},{7,23},{8,24},{9,... | collective-permute-start | bytes 86024 | tf_op jit(solution)/shard_map/ppermute | solution.py:27
  24.8 3.5 %collective-permute-start.13 = (bf16[112,128]{1,0:T(8,128)(2,1)S(1)}, bf16[112,128]{1,0:T(8,128)(2,1)S(1)}, u32[]{:S(2)}, u32[]{:S(2)}) collective-permute-start(bf16[112,128]{1,0:T(8,128)(2,1)S(1)} %get-tuple-element.37), channel_id=1, source_target_pairs={{0,24},{1,25},{2,26},{3,27},{4,28},{5,29},{6,30},{7,31},{8,16},{9,... | collective-permute-start | bytes 86024 | tf_op jit(solution)/shard_map/ppermute | solution.py:27
  28.3 0.7 %shard_map.53 = bf16[2,4,48,128]{3,2,1,0:T(8,128)(2,1)S(1)} custom-call(bf16[2,4,48,128]{3,2,1,0:T(8,128)(2,1)S(1)} %copy-done.2, bf16[4,6,48,128]{3,2,1,0:T(8,128)(2,1)S(1)} %get-tuple-element.24.pad_ref, bf16[192,128]{1,0:T(8,128)(2,1)S(1)} %collective-permute-done.7.outer_ref, bf16[192,128]{1,0:T(8,128)(2,1)S(1)} %collective-permute-done.8.inner_ref, ...), custom_call_target="tpu_custom_call" | custom-call | flops 339738624 | bytes 884736 | tf_op jit(solution)/shard_map/pallas_call | solution.py:56
  29.0 0.6 %copy.5 = bf16[2,4,48,128]{3,2,1,0:T(8,128)(2,1)} copy(bf16[2,4,48,128]{3,2,1,0:T(8,128)(2,1)S(1)} %shard_map.53) | data formatting | bytes 196608
  29.7 0.8 %collective-permute-done.13.refs_3_ = bf16[112,128]{1,0:T(8,128)(2,1)S(1)} collective-permute-done((bf16[112,128]{1,0:T(8,128)(2,1)S(1)}, bf16[112,128]{1,0:T(8,128)(2,1)S(1)}, u32[]{:S(2)}, u32[]{:S(2)}) %collective-permute-start.13) | collective-permute-done | bytes 28704 | tf_op jit(solution)/shard_map/ppermute | solution.py:27
  30.5 0.8 %shard_map.56 = f32[27,16,32]{2,1,0:T(8,128)} custom-call(f32[112,128]{1,0:T(8,128)S(1)} %get-tuple-element.34.refs_0_, bf16[112,128]{1,0:T(8,128)(2,1)S(1)} %collective-permute-done.11.refs_1_, bf16[112,128]{1,0:T(8,128)(2,1)S(1)} %collective-permute-done.12.refs_2_, bf16[112,128]{1,0:T(8,128)(2,1)S(1)} %collective-permute-done.13.refs_3_), custom_call_target="tpu_custom_call" | custom-call | bytes 229376 | tf_op jit(solution)/shard_map/pallas_call | solution.py:56
  (10 shorter events, 0.0 us)
Async XLA Ops:
  0.6 20.0 %copy-start.1 = (bf16[2,4,48,128]{3,2,1,0:T(8,128)(2,1)S(1)}, bf16[2,4,48,128]{3,2,1,0:T(8,128)(2,1)}, u32[]{:S(2)}) copy-start(bf16[2,4,48,128]{3,2,1,0:T(8,128)(2,1)} %refs_8_.1) | copy-start | bytes 294916
  2.0 6.7 %collective-permute-start = (bf16[480,128]{1,0:T(8,128)(2,1)S(1)}, bf16[480,128]{1,0:T(8,128)(2,1)S(1)}, u32[]{:S(2)}, u32[]{:S(2)}) collective-permute-start(bf16[480,128]{1,0:T(8,128)(2,1)S(1)} %get-tuple-element.21), channel_id=1, source_target_pairs={{0,2},{1,3},{2,0},{3,1},{4,6},{5,7},{6,4},{7,5},{8,10},{9,11},{10,... | collective-permute-start | bytes 368648 | tf_op jit(solution)/shard_map/ppermute | solution.py:27
  5.1 7.5 %collective-permute-start.1 = (bf16[480,128]{1,0:T(8,128)(2,1)S(1)}, bf16[480,128]{1,0:T(8,128)(2,1)S(1)}, u32[]{:S(2)}, u32[]{:S(2)}) collective-permute-start(bf16[480,128]{1,0:T(8,128)(2,1)S(1)} %get-tuple-element.22), channel_id=1, source_target_pairs={{0,4},{1,5},{2,6},{3,7},{4,0},{5,1},{6,2},{7,3},{8,12},{9,13},{10,... | collective-permute-start | bytes 368648 | tf_op jit(solution)/shard_map/ppermute | solution.py:27
  6.6 6.0 %collective-permute-start.2 = (bf16[480,128]{1,0:T(8,128)(2,1)S(1)}, bf16[480,128]{1,0:T(8,128)(2,1)S(1)}, u32[]{:S(2)}, u32[]{:S(2)}) collective-permute-start(bf16[480,128]{1,0:T(8,128)(2,1)S(1)} %get-tuple-element.23), channel_id=1, source_target_pairs={{0,6},{1,7},{2,4},{3,5},{4,2},{5,3},{6,0},{7,1},{8,14},{9,15},{10,... | collective-permute-start | bytes 368648 | tf_op jit(solution)/shard_map/ppermute | solution.py:27
  6.6 6.5 %collective-permute-start.3 = (bf16[480,128]{1,0:T(8,128)(2,1)S(1)}, bf16[480,128]{1,0:T(8,128)(2,1)S(1)}, u32[]{:S(2)}, u32[]{:S(2)}) collective-permute-start(bf16[480,128]{1,0:T(8,128)(2,1)S(1)} %get-tuple-element.20.refs_0_), channel_id=1, source_target_pairs={{0,1},{1,0},{2,3},{3,2},{4,5},{5,4},{6,7},{7,6},{8,9},{9,8},{10,11... | collective-permute-start | bytes 368648 | tf_op jit(solution)/shard_map/ppermute | solution.py:27
  8.8 4.3 %collective-permute-start.4 = (bf16[480,128]{1,0:T(8,128)(2,1)S(1)}, bf16[480,128]{1,0:T(8,128)(2,1)S(1)}, u32[]{:S(2)}, u32[]{:S(2)}) collective-permute-start(bf16[480,128]{1,0:T(8,128)(2,1)S(1)} %collective-permute-done.refs_1_), channel_id=1, source_target_pairs={{0,1},{1,0},{2,3},{3,2},{4,5},{5,4},{6,7},{7,6},{8,9},{9,8},{10,11... | collective-permute-start | bytes 368648 | tf_op jit(solution)/shard_map/ppermute | solution.py:27
  12.6 1.3 %collective-permute-start.5 = (bf16[480,128]{1,0:T(8,128)(2,1)S(1)}, bf16[480,128]{1,0:T(8,128)(2,1)S(1)}, u32[]{:S(2)}, u32[]{:S(2)}) collective-permute-start(bf16[480,128]{1,0:T(8,128)(2,1)S(1)} %collective-permute-done.1.refs_2_), channel_id=1, source_target_pairs={{0,1},{1,0},{2,3},{3,2},{4,5},{5,4},{6,7},{7,6},{8,9},{9,8},{10,11... | collective-permute-start | bytes 368648 | tf_op jit(solution)/shard_map/ppermute | solution.py:27
  12.6 1.5 %collective-permute-start.6 = (bf16[480,128]{1,0:T(8,128)(2,1)S(1)}, bf16[480,128]{1,0:T(8,128)(2,1)S(1)}, u32[]{:S(2)}, u32[]{:S(2)}) collective-permute-start(bf16[480,128]{1,0:T(8,128)(2,1)S(1)} %collective-permute-done.2.refs_3_), channel_id=1, source_target_pairs={{0,1},{1,0},{2,3},{3,2},{4,5},{5,4},{6,7},{7,6},{8,9},{9,8},{10,11... | collective-permute-start | bytes 368648 | tf_op jit(solution)/shard_map/ppermute | solution.py:27
  14.4 8.7 %collective-permute-start.9 = (bf16[288,128]{1,0:T(8,128)(2,1)S(1)}, bf16[288,128]{1,0:T(8,128)(2,1)S(1)}, u32[]{:S(2)}, u32[]{:S(2)}) collective-permute-start(bf16[288,128]{1,0:T(8,128)(2,1)S(1)} %get-tuple-element.27), channel_id=1, source_target_pairs={{0,8},{1,9},{2,10},{3,11},{4,12},{5,13},{6,14},{7,15},{8,0},{9,1},... | collective-permute-start | bytes 221192 | tf_op jit(solution)/shard_map/ppermute | solution.py:27
  16.0 7.0 %collective-permute-start.10 = (bf16[288,128]{1,0:T(8,128)(2,1)S(1)}, bf16[288,128]{1,0:T(8,128)(2,1)S(1)}, u32[]{:S(2)}, u32[]{:S(2)}) collective-permute-start(bf16[288,128]{1,0:T(8,128)(2,1)S(1)} %get-tuple-element.28), channel_id=1, source_target_pairs={{0,1},{1,0},{2,3},{3,2},{4,5},{5,4},{6,7},{7,6},{8,16},{9,17},{10,... | collective-permute-start | bytes 221192 | tf_op jit(solution)/shard_map/ppermute | solution.py:27
  16.1 12.2 %collective-permute-start.7 = (bf16[192,128]{1,0:T(8,128)(2,1)S(1)}, bf16[192,128]{1,0:T(8,128)(2,1)S(1)}, u32[]{:S(2)}, u32[]{:S(2)}) collective-permute-start(bf16[192,128]{1,0:T(8,128)(2,1)S(1)} %get-tuple-element.25), channel_id=1, source_target_pairs={{0,1},{1,0},{2,3},{3,2},{4,8},{5,9},{6,10},{7,11},{8,4},{9,5},{10,... | collective-permute-start | bytes 147464 | tf_op jit(solution)/shard_map/ppermute | solution.py:27
  16.5 11.8 %collective-permute-start.8 = (bf16[192,128]{1,0:T(8,128)(2,1)S(1)}, bf16[192,128]{1,0:T(8,128)(2,1)S(1)}, u32[]{:S(2)}, u32[]{:S(2)}) collective-permute-start(bf16[192,128]{1,0:T(8,128)(2,1)S(1)} %get-tuple-element.26), channel_id=1, source_target_pairs={{0,4},{1,5},{2,6},{3,7},{4,0},{5,1},{6,2},{7,3},{8,12},{9,13},{10,... | collective-permute-start | bytes 147464 | tf_op jit(solution)/shard_map/ppermute | solution.py:27
  21.6 6.7 %copy-start = (bf16[27,128,128]{2,1,0:T(8,128)(2,1)S(1)}, bf16[27,128,128]{2,1,0:T(8,128)(2,1)}, u32[]{:S(2)}) copy-start(bf16[27,128,128]{2,1,0:T(8,128)(2,1)} %kernel_ref.1) | copy-start | bytes 2654212
  21.6 6.7 %copy-start.2 = (bf16[2,4,48,128]{3,2,1,0:T(8,128)(2,1)S(1)}, bf16[2,4,48,128]{3,2,1,0:T(8,128)(2,1)}, u32[]{:S(2)}) copy-start(bf16[2,4,48,128]{3,2,1,0:T(8,128)(2,1)} %inputs_ref.1) | copy-start | bytes 294916
  23.8 5.9 %collective-permute-start.11 = (bf16[112,128]{1,0:T(8,128)(2,1)S(1)}, bf16[112,128]{1,0:T(8,128)(2,1)S(1)}, u32[]{:S(2)}, u32[]{:S(2)}) collective-permute-start(bf16[112,128]{1,0:T(8,128)(2,1)S(1)} %get-tuple-element.35), channel_id=1, source_target_pairs={{0,8},{1,9},{2,10},{3,11},{4,12},{5,13},{6,14},{7,15},{8,0},{9,1},... | collective-permute-start | bytes 86024 | tf_op jit(solution)/shard_map/ppermute | solution.py:27
  23.9 5.8 %collective-permute-start.12 = (bf16[112,128]{1,0:T(8,128)(2,1)S(1)}, bf16[112,128]{1,0:T(8,128)(2,1)S(1)}, u32[]{:S(2)}, u32[]{:S(2)}) collective-permute-start(bf16[112,128]{1,0:T(8,128)(2,1)S(1)} %get-tuple-element.36), channel_id=1, source_target_pairs={{0,16},{1,17},{2,18},{3,19},{4,20},{5,21},{6,22},{7,23},{8,24},{9,... | collective-permute-start | bytes 86024 | tf_op jit(solution)/shard_map/ppermute | solution.py:27
  24.8 5.7 %collective-permute-start.13 = (bf16[112,128]{1,0:T(8,128)(2,1)S(1)}, bf16[112,128]{1,0:T(8,128)(2,1)S(1)}, u32[]{:S(2)}, u32[]{:S(2)}) collective-permute-start(bf16[112,128]{1,0:T(8,128)(2,1)S(1)} %get-tuple-element.37), channel_id=1, source_target_pairs={{0,24},{1,25},{2,26},{3,27},{4,28},{5,29},{6,30},{7,31},{8,16},{9,... | collective-permute-start | bytes 86024 | tf_op jit(solution)/shard_map/ppermute | solution.py:27
